TPU v7x, 32 devices: a whole 2x2x4 slice. The times are simulated.
32 devices in a mesh: dp: 8 (over y, x, core), tensor: 4 (over z).
Axes of the slice: x: 2, y: 2, z: 4, core: 2. Of those that a mesh axis runs over, the one named last changes fastest.
Arguments:
- block_in: bfloat16 [8192, 4096], P(('dp', 'tensor')), may hold values from -6 to 6
- out_grad: bfloat16 [8192, 4096], P(('dp', 'tensor')), may hold values from -6 to 6
- segment_ids: int32 [8192], P('dp'), may hold values from 0 to 2, as said below
- positions: int32 [8192], P('dp'), may hold values from 0 to 1023, as said below
- group_token_counts: int32 [8], P('dp'), may hold values from 512 to 1024, as said below
- gain_attn: float32 [4096], replicated, may hold values from 0.1 to 1.9
- w_query: bfloat16 [4096, 4096], P('dp', 'tensor'), may hold values from -0.3125 to 0.3125
- w_key: bfloat16 [4096, 4096], P('dp', 'tensor'), may hold values from -0.3125 to 0.3125
- w_value: bfloat16 [4096, 4096], P('dp', 'tensor'), may hold values from -0.09375 to 0.09375
- w_out: bfloat16 [4096, 4096], P('tensor', 'dp'), may hold values from -0.5 to 0.5
- gain_mlp: float32 [4096], replicated, may hold values from 0.1 to 1.9
- w_gate: bfloat16 [4096, 11008], P('dp', 'tensor'), may hold values from -0.09375 to 0.09375
- w_up: bfloat16 [4096, 11008], P('dp', 'tensor'), may hold values from -0.09375 to 0.09375
- w_down: bfloat16 [11008, 4096], P('tensor', 'dp'), may hold values from -0.0546875 to 0.0546875
Outputs:
- block_out: bfloat16 [8192, 4096], P(('dp', 'tensor'))
- input_grad: bfloat16 [8192, 4096], P(('dp', 'tensor'))
- grad_gain_attn: float32 [4096], replicated
- grad_query: float32 [4096, 4096], P('dp', 'tensor')
- grad_key: float32 [4096, 4096], P('dp', 'tensor')
- grad_value: float32 [4096, 4096], P('dp', 'tensor')
- grad_out: float32 [4096, 4096], P('tensor', 'dp')
- grad_gain_mlp: float32 [4096], replicated
- grad_gate: float32 [4096, 11008], P('dp', 'tensor')
- grad_up: float32 [4096, 11008], P('dp', 'tensor')
- grad_down: float32 [11008, 4096], P('tensor', 'dp')
Inputs may be any that keep to these rules, and one draw needn't show every extreme that they name: `segment_ids`: within each group of 1024 rows segment ids never fall; ids 0 and 1 are the group's sequences (1 may be absent) and 2 marks the rows from group_token_counts of that group on, when there are any. In a group whose live rows number 1024 or more, sequence 0 holds at least 1024 rows; otherwise it holds all live rows. Each segment's positions run 0, 1, 2, ... in row order. In every draw some group is one sequence of all 1024 rows. `group_token_counts`: some group is full in every draw.
All inputs are finite; a program needn't handle non-finite values.
Results may differ from a plain program's by a relative error of at most 0.014.
Values may be sent and summed in bfloat16 or wider, within the bound.
No kernel may reach another device: no remote copies, remote signals or barrier semaphores. Data moves between devices by JAX's collectives and lax.ppermute only.
A program may use at most 448 MiB of HBM per device.

v0:
```python
import jax
import jax.numpy as jnp
from jax import lax
from jax.sharding import PartitionSpec as P

QBLOCKS = 4
HEAD_DIM = 128


EPSILON = 1e-05
ROPE_BASE = 10000.0


def matmul(left, right):
    return jnp.dot(left, right, preferred_element_type=jnp.float32)


def left_t(left, right):
    return lax.dot_general(
        left, right, (((0,), (0,)), ((), ())), preferred_element_type=jnp.float32
    )


def right_t(left, right):
    return lax.dot_general(
        left, right, (((1,), (1,)), ((), ())), preferred_element_type=jnp.float32
    )


def rope_tables(position):
    half_dim = HEAD_DIM // 2
    freq_index = jnp.arange(half_dim).astype(jnp.float32)
    frequency = ROPE_BASE ** (-2.0 * freq_index / HEAD_DIM)
    angles = position.astype(jnp.float32)[:, None] * frequency[None, :]
    cos_tab = jnp.cos(angles)
    sine_tab = jnp.sin(angles)
    return (
        jnp.concatenate([cos_tab, cos_tab], 1)[:, None, :],
        jnp.concatenate([sine_tab, sine_tab], 1)[:, None, :],
    )


def rotate(field):
    half_dim = field.shape[-1] // 2
    return jnp.concatenate([-field[..., half_dim:], field[..., :half_dim]], -1)


def rotate_back(field):
    half_dim = field.shape[-1] // 2
    return jnp.concatenate([field[..., half_dim:], -field[..., :half_dim]], -1)


def apply_rope(field, cos_tab, sine_tab):
    return field * cos_tab + rotate(field) * sine_tab


def undo_rope(field, cos_tab, sine_tab):
    return field * cos_tab + rotate_back(field * sine_tab)


def norm_back(layer_in, row_inverse_scale, norm_weight, normalized_gradient):
    standardized_gradient = normalized_gradient * norm_weight
    standardized_rows = layer_in * row_inverse_scale
    layer_gradient = row_inverse_scale * (
        standardized_gradient
        - standardized_rows
        * jnp.mean(standardized_gradient * standardized_rows, axis=1, keepdims=True)
    )
    return (layer_gradient, jnp.sum(normalized_gradient * standardized_rows, axis=0))


def shards(
    block_in,
    out_grad,
    segment_ids,
    positions,
    group_token_counts,
    gain_attn,
    w_query,
    w_key,
    w_value,
    w_out,
    gain_mlp,
    w_gate,
    w_up,
    w_down,
):
    tok_rows = block_in.shape[0]
    query_all, key_all, value_all, out_all = (
        lax.all_gather(w_query, "dp", axis=0, tiled=True),
        lax.all_gather(w_key, "dp", axis=0, tiled=True),
        lax.all_gather(w_value, "dp", axis=0, tiled=True),
        lax.all_gather(w_out, "dp", axis=1, tiled=True),
    )
    gate_all, up_all, down_all = (
        lax.all_gather(w_gate, "dp", axis=0, tiled=True),
        lax.all_gather(w_up, "dp", axis=0, tiled=True),
        lax.all_gather(w_down, "dp", axis=1, tiled=True),
    )
    x_float = block_in.astype(jnp.float32)
    attn_scale = lax.rsqrt(jnp.mean(x_float * x_float, axis=1, keepdims=True) + EPSILON)
    attn_normed = (x_float * attn_scale * gain_attn).astype(jnp.bfloat16)
    whole_attn = lax.all_gather(attn_normed, "tensor", axis=0, tiled=True)
    group_rows = whole_attn.shape[0]
    local_heads = query_all.shape[1] // HEAD_DIM
    cos_tab, sine_tab = rope_tables(positions)

    def split_heads(field):
        return field.reshape(group_rows, local_heads, HEAD_DIM)

    queries = apply_rope(split_heads(matmul(whole_attn, query_all)), cos_tab, sine_tab).astype(
        jnp.bfloat16
    )
    keys_all = apply_rope(split_heads(matmul(whole_attn, key_all)), cos_tab, sine_tab).astype(
        jnp.bfloat16
    )
    values = split_heads(matmul(whole_attn, value_all)).astype(jnp.bfloat16)
    block_rows = group_rows // QBLOCKS
    row_order = jnp.arange(group_rows)
    score_scale = HEAD_DIM ** (-0.5)

    def block_scores(block_index):
        low_row = block_index * block_rows
        high_row = low_row + block_rows
        scores = (
            jnp.einsum(
                "qhd,khd->hqk",
                queries[low_row:high_row],
                keys_all[:high_row],
                preferred_element_type=jnp.float32,
            )
            * score_scale
        )
        allowed = (segment_ids[low_row:high_row, None] == segment_ids[None, :high_row]) & (
            row_order[None, :high_row] <= row_order[low_row:high_row, None]
        )
        return jnp.where(allowed[None], scores, -1e30)

    attn_parts = []
    total_parts = []
    for block_index in range(QBLOCKS):
        high_row = (block_index + 1) * block_rows
        scores = block_scores(block_index)
        row_max = jnp.max(scores, axis=2, keepdims=True)
        log_total = row_max + jnp.log(jnp.sum(jnp.exp(scores - row_max), axis=2, keepdims=True))
        prob_bf = jnp.exp(scores - log_total).astype(jnp.bfloat16)
        attn_parts.append(
            jnp.einsum(
                "hqk,khd->qhd", prob_bf, values[:high_row], preferred_element_type=jnp.float32
            ).astype(jnp.bfloat16)
        )
        total_parts.append(log_total)
    attn_heads = jnp.concatenate(attn_parts, 0)
    attn = attn_heads.reshape(group_rows, local_heads * HEAD_DIM)
    resid = x_float + lax.psum_scatter(
        matmul(attn, out_all), "tensor", scatter_dimension=0, tiled=True
    )
    mlp_scale = lax.rsqrt(jnp.mean(resid * resid, axis=1, keepdims=True) + EPSILON)
    mlp_normed = (resid * mlp_scale * gain_mlp).astype(jnp.bfloat16)
    whole_mlp = lax.all_gather(mlp_normed, "tensor", axis=0, tiled=True)
    gate_pre = matmul(whole_mlp, gate_all)
    up_pre = matmul(whole_mlp, up_all)
    sigmoid_gate = jax.nn.sigmoid(gate_pre)
    silu_gate = gate_pre * sigmoid_gate
    hidden = (silu_gate * up_pre).astype(jnp.bfloat16)
    block_out = (
        resid
        + lax.psum_scatter(
            matmul(hidden, down_all).astype(jnp.bfloat16), "tensor", scatter_dimension=0, tiled=True
        ).astype(jnp.float32)
    ).astype(jnp.bfloat16)
    first_live = lax.axis_index("tensor") * tok_rows
    live = (first_live + jnp.arange(tok_rows) < group_token_counts[0]).astype(jnp.bfloat16)
    live_grad = out_grad * live[:, None]
    whole_grad = lax.all_gather(live_grad, "tensor", axis=0, tiled=True)
    d_hidden = right_t(whole_grad, down_all)
    grad_down_part = left_t(hidden, whole_grad)
    d_gate = (d_hidden * up_pre * sigmoid_gate * (1.0 + gate_pre * (1.0 - sigmoid_gate))).astype(
        jnp.bfloat16
    )
    d_up = (d_hidden * silu_gate).astype(jnp.bfloat16)
    grad_gate_part = left_t(whole_mlp, d_gate)
    grad_up_part = left_t(whole_mlp, d_up)
    d_norm_mlp = lax.psum_scatter(
        right_t(d_gate, gate_all) + right_t(d_up, up_all), "tensor", scatter_dimension=0, tiled=True
    )
    d_from_mlp, gain_mlp_part = norm_back(resid, mlp_scale, gain_mlp, d_norm_mlp)
    d_resid = live_grad.astype(jnp.float32) + d_from_mlp
    d_resid_b = d_resid.astype(jnp.bfloat16)
    whole_resid = lax.all_gather(d_resid_b, "tensor", axis=0, tiled=True)
    grad_out_part = left_t(attn, whole_resid)
    d_attn = split_heads(right_t(whole_resid, out_all).astype(jnp.bfloat16))
    d_q_parts = []
    d_key_sum = jnp.zeros((group_rows, local_heads, HEAD_DIM), jnp.float32)
    d_value_sum = jnp.zeros((group_rows, local_heads, HEAD_DIM), jnp.float32)
    for block_index in range(QBLOCKS):
        low_row = block_index * block_rows
        high_row = low_row + block_rows
        scores = block_scores(block_index)
        prob_full = jnp.exp(scores - total_parts[block_index])
        dout_rows = d_attn[low_row:high_row]
        row_delta = jnp.sum(
            dout_rows.astype(jnp.float32) * attn_heads[low_row:high_row].astype(jnp.float32), axis=2
        )
        row_delta = jnp.swapaxes(row_delta, 0, 1)[:, :, None]
        d_probs = jnp.einsum(
            "qhd,khd->hqk", dout_rows, values[:high_row], preferred_element_type=jnp.float32
        )
        d_scores = (prob_full * (d_probs - row_delta) * score_scale).astype(jnp.bfloat16)
        d_value_sum = d_value_sum.at[:high_row].add(
            jnp.einsum(
                "hqk,qhd->khd",
                prob_full.astype(jnp.bfloat16),
                dout_rows,
                preferred_element_type=jnp.float32,
            )
        )
        d_q_parts.append(
            jnp.einsum(
                "hqk,khd->qhd", d_scores, keys_all[:high_row], preferred_element_type=jnp.float32
            )
        )
        d_key_sum = d_key_sum.at[:high_row].add(
            jnp.einsum(
                "hqk,qhd->khd",
                d_scores,
                queries[low_row:high_row],
                preferred_element_type=jnp.float32,
            )
        )
    local_width = local_heads * HEAD_DIM
    d_queries = (
        undo_rope(jnp.concatenate(d_q_parts, 0), cos_tab, sine_tab)
        .astype(jnp.bfloat16)
        .reshape(group_rows, local_width)
    )
    d_keys = (
        undo_rope(d_key_sum, cos_tab, sine_tab)
        .astype(jnp.bfloat16)
        .reshape(group_rows, local_width)
    )
    d_values = d_value_sum.astype(jnp.bfloat16).reshape(group_rows, local_width)
    grad_query_part = left_t(whole_attn, d_queries)
    grad_key_part = left_t(whole_attn, d_keys)
    grad_value_part = left_t(whole_attn, d_values)
    d_norm_attn = lax.psum_scatter(
        right_t(d_queries, query_all) + right_t(d_keys, key_all) + right_t(d_values, value_all),
        "tensor",
        scatter_dimension=0,
        tiled=True,
    )
    d_from_attn, gain_attn_part = norm_back(x_float, attn_scale, gain_attn, d_norm_attn)
    input_grad = (d_resid + d_from_attn).astype(jnp.bfloat16)
    grad_query, grad_key, grad_value, grad_out, grad_gate, grad_up, grad_down = (
        lax.psum_scatter(grad_query_part, "dp", scatter_dimension=0, tiled=True),
        lax.psum_scatter(grad_key_part, "dp", scatter_dimension=0, tiled=True),
        lax.psum_scatter(grad_value_part, "dp", scatter_dimension=0, tiled=True),
        lax.psum_scatter(grad_out_part, "dp", scatter_dimension=1, tiled=True),
        lax.psum_scatter(grad_gate_part, "dp", scatter_dimension=0, tiled=True),
        lax.psum_scatter(grad_up_part, "dp", scatter_dimension=0, tiled=True),
        lax.psum_scatter(grad_down_part, "dp", scatter_dimension=1, tiled=True),
    )
    grad_gain_attn, grad_gain_mlp = lax.psum((gain_attn_part, gain_mlp_part), ("dp", "tensor"))
    return (
        block_out,
        input_grad,
        grad_gain_attn,
        grad_query,
        grad_key,
        grad_value,
        grad_out,
        grad_gain_mlp,
        grad_gate,
        grad_up,
        grad_down,
    )


def solution(mesh):
    placed = (
        P(("dp", "tensor"), None),
        P(("dp", "tensor"), None),
        P("dp"),
        P("dp"),
        P("dp"),
        P(),
        P("dp", "tensor"),
        P("dp", "tensor"),
        P("dp", "tensor"),
        P("tensor", "dp"),
        P(),
        P("dp", "tensor"),
        P("dp", "tensor"),
        P("tensor", "dp"),
    )
    return jax.shard_map(
        shards,
        mesh=mesh,
        in_specs=placed,
        out_specs=(
            P(("dp", "tensor"), None),
            P(("dp", "tensor"), None),
            P(),
            P("dp", "tensor"),
            P("dp", "tensor"),
            P("dp", "tensor"),
            P("tensor", "dp"),
            P(),
            P("dp", "tensor"),
            P("dp", "tensor"),
            P("tensor", "dp"),
        ),
        check_vma=False,
    )
```

profile of v0, /device:TPU:0, one launch (start us, length us, event | category | flops | bytes accessed | tf_op | source)
XLA Modules:
  0.0 3740.4 jit_solution(11734040073000018754)
XLA Ops:
  22.3 143.7 %all-gather.12.cloned.1.call-done = bf16[1024,4096]{1,0:T(8,128)(2,1)} async-done(((bf16[256,4096]{1,0:T(8,128)(2,1)}), bf16[1024,4096]{1,0:T(8,128)(2,1)}) %all-gather.12.cloned.1.call-update) | async-done | bytes 8388624 | tf_op jit(solution)/shard_map/all_gather | solution.py:103
  166.0 54.5 %all-gather.14.cloned.1.call-done = bf16[4096,1024]{1,0:T(8,128)(2,1)} async-done(((bf16[512,1024]{1,0:T(8,128)(2,1)}), bf16[4096,1024]{1,0:T(8,128)(2,1)}) %all-gather.14.cloned.1.call-update) | async-done | bytes 8388624 | tf_op jit(solution)/shard_map/all_gather | solution.py:92
  237.1 39.7 %all-gather.16.cloned.1.call-done = bf16[4096,1024]{1,0:T(8,128)(2,1)} async-done(((bf16[512,1024]{1,0:T(8,128)(2,1)}), bf16[4096,1024]{1,0:T(8,128)(2,1)}) %all-gather.16.cloned.1.call-update) | async-done | bytes 8388624 | tf_op jit(solution)/shard_map/all_gather | solution.py:90
  297.2 35.8 all-gather.18.cloned.1.call-done
  406.3 279.6 %reduce-scatter.12.cloned.1.call-done = f32[256,4096]{1,0:T(8,128)} async-done(((f32[1024,4096]{1,0:T(8,128)}), f32[256,4096]{1,0:T(8,128)}) %reduce-scatter.12.cloned.1.call-update) | async-done | bytes 4194320 | tf_op jit(solution)/shard_map/reduce_scatter | solution.py:155
  697.1 110.3 %all-gather.24.cloned.1.call-done = bf16[4096,2752]{0,1:T(8,128)(2,1)} async-done(((bf16[512,2752]{0,1:T(8,128)(2,1)}), bf16[4096,2752]{0,1:T(8,128)(2,1)}) %all-gather.24.cloned.1.call-update) | async-done | bytes 22544400 | tf_op jit(solution)/shard_map/all_gather | solution.py:96
  807.4 151.9 %all-gather.22.cloned.1.call-done = bf16[1024,4096]{1,0:T(8,128)(2,1)} async-done(((bf16[256,4096]{1,0:T(8,128)(2,1)}), bf16[1024,4096]{1,0:T(8,128)(2,1)}) %all-gather.22.cloned.1.call-update) | async-done | bytes 8388624 | tf_op jit(solution)/shard_map/all_gather | solution.py:160
  990.1 88.2 %all-gather.26.cloned.1.call-done = bf16[4096,2752]{0,1:T(8,128)(2,1)} async-done(((bf16[512,2752]{0,1:T(8,128)(2,1)}), bf16[4096,2752]{0,1:T(8,128)(2,1)}) %all-gather.26.cloned.1.call-update) | async-done | bytes 22544400 | tf_op jit(solution)/shard_map/all_gather | solution.py:97
  1108.9 121.1 %all-gather.30.cloned.1.call-done = bf16[1024,4096]{1,0:T(8,128)(2,1)} async-done(((bf16[256,4096]{1,0:T(8,128)(2,1)}), bf16[1024,4096]{1,0:T(8,128)(2,1)}) %all-gather.30.cloned.1.call-update) | async-done | bytes 8388624 | tf_op jit(solution)/shard_map/all_gather | solution.py:175
  1230.0 119.0 %all-gather.28.cloned.1.call-done = bf16[2752,4096]{1,0:T(8,128)(2,1)} async-done(((bf16[2752,512]{1,0:T(8,128)(2,1)}), bf16[2752,4096]{1,0:T(8,128)(2,1)}) %all-gather.28.cloned.1.call-update) | async-done | bytes 22544400 | tf_op jit(solution)/shard_map/all_gather | solution.py:98
  1349.0 38.0 %multiply_convert_fusion = (bf16[1024,2752]{0,1:T(8,128)(2,1)}, bf16[1024,2752]{0,1:T(8,128)(2,1)}, bf16[1024,2752]{0,1:T(8,128)(2,1)}) fusion(f32[1024,2752]{0,1:T(8,128)} %fusion.75, f32[1024,2752]{0,1:T(8,128)} %fusion.76, bf16[1024,4096]{1,0:T(8,128)(2,1)} %all-gather.30.cloned.1.call-done, bf16[2752,4096]{1,0:T(8,128)(2,1)} %all-gather.28.cloned.1.call-done), kind=kOutput, calls=%fused_computation.1 | convolution fusion | flops 23127719936 | bytes 70385664 | tf_op jit(solution)/shard_map/dot_general | solution.py:25
  1417.1 32.0 convolution_add_fusion
  1449.2 280.4 %reduce-scatter.16.cloned.1.call-done = f32[256,4096]{1,0:T(8,128)} async-done(((f32[1024,4096]{1,0:T(8,128)}), f32[256,4096]{1,0:T(8,128)}) %reduce-scatter.16.cloned.1.call-update) | async-done | bytes 4194320 | tf_op jit(solution)/shard_map/reduce_scatter | solution.py:184
  1739.5 149.5 %all-gather.32.cloned.1.call-done = bf16[1024,4096]{1,0:T(8,128)(2,1)} async-done(((bf16[256,4096]{1,0:T(8,128)(2,1)}), bf16[1024,4096]{1,0:T(8,128)(2,1)}) %all-gather.32.cloned.1.call-update) | async-done | bytes 8388624 | tf_op jit(solution)/shard_map/all_gather | solution.py:190
  2225.0 86.5 %reduce-scatter.18.cloned.1.call-done = f32[256,4096]{1,0:T(8,128)} async-done(((f32[1024,4096]{1,0:T(8,128)}), f32[256,4096]{1,0:T(8,128)}) %reduce-scatter.18.cloned.1.call-update) | async-done | bytes 4194320 | tf_op jit(solution)/shard_map/reduce_scatter | solution.py:246
  2314.9 46.8 %all-reduce.2 = (f32[4096]{0:T(1024)}, f32[4096]{0:T(1024)}) all-reduce(f32[4096]{0:T(1024)S(1)} %get-tuple-element.125, f32[4096]{0:T(1024)S(1)} %copy-done.65), channel_id=1, replica_groups=mesh['dp'=8,'tensor'=4] {'dp','tensor'}, use_global_device_ids=true, to_apply=%region_21.22 | all-reduce | flops 8192 | bytes 65536 | tf_op jit(solution)/shard_map/psum | solution.py:263
  2361.7 98.3 %reduce-scatter.14.cloned.1.call-done = bf16[256,4096]{1,0:T(8,128)(2,1)} async-done(((bf16[1024,4096]{1,0:T(8,128)(2,1)}), bf16[256,4096]{1,0:T(8,128)(2,1)}) %reduce-scatter.14.cloned.1.call-update) | async-done | bytes 2097168 | tf_op jit(solution)/shard_map/reduce_scatter | solution.py:168
  2468.7 255.4 %reduce-scatter.28.cloned.1.call-done = f32[512,2752]{0,1:T(8,128)} async-done(((f32[4096,2752]{0,1:T(8,128)}), f32[512,2752]{0,1:T(8,128)}) %reduce-scatter.28.cloned.1.call-update) | async-done | bytes 5636112 | tf_op jit(solution)/shard_map/reduce_scatter | solution.py:259
  2724.1 263.4 %reduce-scatter.30.cloned.1.call-done = f32[512,2752]{0,1:T(8,128)} async-done(((f32[4096,2752]{0,1:T(8,128)}), f32[512,2752]{0,1:T(8,128)}) %reduce-scatter.30.cloned.1.call-update) | async-done | bytes 5636112 | tf_op jit(solution)/shard_map/reduce_scatter | solution.py:260
  2987.5 263.5 %reduce-scatter.32.cloned.1.call-done = f32[2752,512]{1,0:T(8,128)} async-done(((f32[2752,4096]{1,0:T(8,128)}), f32[2752,512]{1,0:T(8,128)}) %reduce-scatter.32.cloned.1.call-update) | async-done | bytes 5636112 | tf_op jit(solution)/shard_map/reduce_scatter | solution.py:261
  3251.0 120.6 %reduce-scatter.24.cloned.1.call-done = f32[512,1024]{1,0:T(8,128)} async-done(((f32[4096,1024]{1,0:T(8,128)}), f32[512,1024]{1,0:T(8,128)}) %reduce-scatter.24.cloned.1.call-update) | async-done | bytes 2097168 | tf_op jit(solution)/shard_map/reduce_scatter | solution.py:257
  3371.6 120.4 %reduce-scatter.22.cloned.1.call-done = f32[512,1024]{1,0:T(8,128)} async-done(((f32[4096,1024]{1,0:T(8,128)}), f32[512,1024]{1,0:T(8,128)}) %reduce-scatter.22.cloned.1.call-update) | async-done | bytes 2097168 | tf_op jit(solution)/shard_map/reduce_scatter | solution.py:256
  3492.0 120.6 %reduce-scatter.26.cloned.1.call-done = f32[1024,512]{1,0:T(8,128)} async-done(((f32[1024,4096]{1,0:T(8,128)}), f32[1024,512]{1,0:T(8,128)}) %reduce-scatter.26.cloned.1.call-update) | async-done | bytes 2097168 | tf_op jit(solution)/shard_map/reduce_scatter | solution.py:258
  3612.5 120.6 %reduce-scatter.20.cloned.1.call-done = f32[512,1024]{1,0:T(8,128)} async-done(((f32[4096,1024]{1,0:T(8,128)}), f32[512,1024]{1,0:T(8,128)}) %reduce-scatter.20.cloned.1.call-update) | async-done | bytes 2097168 | tf_op jit(solution)/shard_map/reduce_scatter | solution.py:255
  (335 shorter events, 584.1 us)
Async XLA Ops:
  7.2 158.8 %all-gather.12.cloned.1.call-start = ((), (), s32[]{:S(2)}) async-start(), calls=%async_computation.11 | async-start | bytes 10485760 | tf_op jit(solution)/shard_map/all_gather | solution.py:103
  13.5 207.0 %all-gather.14.cloned.1.call-start = ((), (), s32[]{:S(2)}) async-start(), calls=%async_computation.12 | async-start | bytes 9437184 | tf_op jit(solution)/shard_map/all_gather | solution.py:92
  14.2 262.6 %all-gather.16.cloned.1.call-start = ((), (), s32[]{:S(2)}) async-start(), calls=%async_computation.13 | async-start | bytes 9437184 | tf_op jit(solution)/shard_map/all_gather | solution.py:90
  15.0 318.0 %all-gather.18.cloned.1.call-start = ((), (), s32[]{:S(2)}) async-start(), calls=%async_computation.14 | async-start | bytes 9437184 | tf_op jit(solution)/shard_map/all_gather | solution.py:91
  15.5 375.2 %all-gather.20.cloned.1.call-start = ((), (), s32[]{:S(2)}) async-start(), calls=%async_computation.15 | async-start | bytes 9437184 | tf_op jit(solution)/shard_map/all_gather | solution.py:93
  16.1 669.8 %reduce-scatter.12.cloned.1.call-start = ((), (), s32[]{:S(2)}) async-start(), calls=%async_computation.16 | async-start | bytes 20971520 | tf_op jit(solution)/shard_map/reduce_scatter | solution.py:155
  20.2 341.8 %copy-start.20 = (f32[1024,128]{1,0:T(8,128)}, f32[1024,128]{1,0:T(8,128)S(1)}, u32[]{:S(2)}) copy-start(f32[1024,128]{1,0:T(8,128)S(1)} %get-tuple-element.171) | copy-start | bytes 1572868
  20.2 341.8 %copy-start.30 = (f32[1024,128]{1,0:T(8,128)}, f32[1024,128]{1,0:T(8,128)S(1)}, u32[]{:S(2)}) copy-start(f32[1024,128]{1,0:T(8,128)S(1)} %get-tuple-element.172) | copy-start | bytes 1572868
  405.5 401.9 %all-gather.24.cloned.1.call-start = ((), (), s32[]{:S(2)}) async-start(), calls=%async_computation.18 | async-start | bytes 25362432 | tf_op jit(solution)/shard_map/all_gather | solution.py:96
  406.3 553.0 %all-gather.22.cloned.1.call-start = ((), (), s32[]{:S(2)}) async-start(), calls=%async_computation.17 | async-start | bytes 10485760 | tf_op jit(solution)/shard_map/all_gather | solution.py:160
  692.7 385.6 %all-gather.26.cloned.1.call-start = ((), (), s32[]{:S(2)}) async-start(), calls=%async_computation.19 | async-start | bytes 25362432 | tf_op jit(solution)/shard_map/all_gather | solution.py:97
  693.4 536.6 %all-gather.30.cloned.1.call-start = ((), (), s32[]{:S(2)}) async-start(), calls=%async_computation.22 | async-start | bytes 10485760 | tf_op jit(solution)/shard_map/all_gather | solution.py:175
  696.3 652.7 %all-gather.28.cloned.1.call-start = ((), (), s32[]{:S(2)}) async-start(), calls=%async_computation.20 | async-start | bytes 25362432 | tf_op jit(solution)/shard_map/all_gather | solution.py:98
  697.0 1032.6 %reduce-scatter.16.cloned.1.call-start = ((), (), s32[]{:S(2)}) async-start(), calls=%async_computation.23 | async-start | bytes 20971520 | tf_op jit(solution)/shard_map/reduce_scatter | solution.py:184
  1449.2 439.8 %all-gather.32.cloned.1.call-start = ((), (), s32[]{:S(2)}) async-start(), calls=%async_computation.24 | async-start | bytes 10485760 | tf_op jit(solution)/shard_map/all_gather | solution.py:190
  1738.5 573.0 %reduce-scatter.18.cloned.1.call-start = ((), (), s32[]{:S(2)}) async-start(), calls=%async_computation.25 | async-start | bytes 20971520 | tf_op jit(solution)/shard_map/reduce_scatter | solution.py:246
  2032.8 427.2 %reduce-scatter.14.cloned.1.call-start = ((), (), s32[]{:S(2)}) async-start(), calls=%async_computation.21 | async-start | bytes 10485760 | tf_op jit(solution)/shard_map/reduce_scatter | solution.py:168
  2064.4 659.7 %reduce-scatter.28.cloned.1.call-start = ((), (), s32[]{:S(2)}) async-start(), calls=%async_computation.30 | async-start | bytes 50724864 | tf_op jit(solution)/shard_map/reduce_scatter | solution.py:259
  2096.1 891.5 %reduce-scatter.30.cloned.1.call-start = ((), (), s32[]{:S(2)}) async-start(), calls=%async_computation.31 | async-start | bytes 50724864 | tf_op jit(solution)/shard_map/reduce_scatter | solution.py:260
  2128.0 1123.0 %reduce-scatter.32.cloned.1.call-start = ((), (), s32[]{:S(2)}) async-start(), calls=%async_computation.32 | async-start | bytes 50724864 | tf_op jit(solution)/shard_map/reduce_scatter | solution.py:261
  2159.7 1211.9 %reduce-scatter.24.cloned.1.call-start = ((), (), s32[]{:S(2)}) async-start(), calls=%async_computation.28 | async-start | bytes 18874368 | tf_op jit(solution)/shard_map/reduce_scatter | solution.py:257
  2176.1 1315.9 %reduce-scatter.22.cloned.1.call-start = ((), (), s32[]{:S(2)}) async-start(), calls=%async_computation.27 | async-start | bytes 18874368 | tf_op jit(solution)/shard_map/reduce_scatter | solution.py:256
  2192.4 1420.2 %reduce-scatter.26.cloned.1.call-start = ((), (), s32[]{:S(2)}) async-start(), calls=%async_computation.29 | async-start | bytes 18874368 | tf_op jit(solution)/shard_map/reduce_scatter | solution.py:258
  2208.7 1524.4 %reduce-scatter.20.cloned.1.call-start = ((), (), s32[]{:S(2)}) async-start(), calls=%async_computation.26 | async-start | bytes 18874368 | tf_op jit(solution)/shard_map/reduce_scatter | solution.py:255
  (88 other events, 3409.0 us)
Sparse Core Ops, SparseCore 0:
  13.6 152.3 all-gather.11
  167.8 52.6 all-gather.13
  222.4 54.3 all-gather.15
  278.6 54.3 all-gather.17
  334.7 55.9 all-gather.19
  405.6 280.2 reduce-scatter.11
  688.0 119.3 all-gather.23
  809.6 149.6 all-gather.21
  961.3 116.8 all-gather.25
  1080.3 149.6 all-gather.29
  1232.0 116.8 all-gather.27
  1449.3 280.2 reduce-scatter.15
  1738.6 150.3 all-gather.31
  2032.9 278.5 reduce-scatter.17
  2313.8 146.1 reduce-scatter.13
  2464.6 259.4 reduce-scatter.27
  2728.7 258.7 reduce-scatter.29
  2992.2 258.7 reduce-scatter.31
  3255.6 115.9 reduce-scatter.23
  3376.0 115.9 reduce-scatter.21
  3496.5 115.9 reduce-scatter.25
  3617.1 115.9 reduce-scatter.19
where the time goes:
time: 3750 us; the launch traced here: 3740 us
  waiting for transfers between devices  3030 us (81%)
  matrix products  521 us (14%)
  other arithmetic  75.1 us (2%)
  local copies, waits for them, and re-layouts  50.8 us (1%)
  blocking collectives  46.8 us (1%)
    reduce_scatter x1, waiting for transfers between devices, shards(): lax.psum_scatter(right_t(d_gate, gate_all) + right_t(d_up, up_all), 'tens...  280 us
    reduce_scatter x1, waiting for transfers between devices, shards(): lax.psum_scatter(matmul(attn, out_all), 'tensor', scatter_dimension=0, ti...  280 us
    reduce_scatter x1, waiting for transfers between devices, shards(): lax.psum_scatter(grad_down_part, 'dp', scatter_dimension=1, tiled=True)  263 us
    reduce_scatter x1, waiting for transfers between devices, shards(): lax.psum_scatter(grad_up_part, 'dp', scatter_dimension=0, tiled=True)  263 us
    reduce_scatter x1, waiting for transfers between devices, shards(): lax.psum_scatter(grad_gate_part, 'dp', scatter_dimension=0, tiled=True)  255 us
    dot_general x7, matrix products, right_t(): lax.dot_general(left, right, (((1,), (1,)), ((), ())), preferred_element_...  166 us
    dot_general x7, matrix products, left_t(): lax.dot_general(left, right, (((0,), (0,)), ((), ())), preferred_element_...  154 us
    dot_general x7, matrix products, matmul(): return jnp.dot(left, right, preferred_element_type=jnp.float32)  152 us
  transfers between devices with their start and end apart: 22, of which 22 were waited for; matrix products, arithmetic and copies ran while one was open for 10% of the time, Pallas kernels for 0%

commit v1 on v0

v1 whole, which is shorter than its diff:
```python
import jax
import jax.numpy as jnp
from jax import lax
from jax.sharding import PartitionSpec as P

QBLOCKS = 4
HEAD_DIM = 128
EPSILON = 1e-05
ROPE_BASE = 10000.0
BF16 = jnp.bfloat16
F32 = jnp.float32


def matmul(left, right):
    return jnp.dot(left, right, preferred_element_type=F32)


def left_t(left, right):
    return lax.dot_general(left, right, (((0,), (0,)), ((), ())), preferred_element_type=F32)


def right_t(left, right):
    return lax.dot_general(left, right, (((1,), (1,)), ((), ())), preferred_element_type=F32)


def rope_tables(position):
    half_dim = HEAD_DIM // 2
    freq_index = jnp.arange(half_dim).astype(F32)
    frequency = ROPE_BASE ** (-2.0 * freq_index / HEAD_DIM)
    angles = position.astype(F32)[:, None] * frequency[None, :]
    cos_tab = jnp.cos(angles)
    sine_tab = jnp.sin(angles)
    return (
        jnp.concatenate([cos_tab, cos_tab], 1)[:, None, :],
        jnp.concatenate([sine_tab, sine_tab], 1)[:, None, :],
    )


def rotate(field):
    half_dim = field.shape[-1] // 2
    return jnp.concatenate([-field[..., half_dim:], field[..., :half_dim]], -1)


def rotate_back(field):
    half_dim = field.shape[-1] // 2
    return jnp.concatenate([field[..., half_dim:], -field[..., :half_dim]], -1)


def apply_rope(field, cos_tab, sine_tab):
    return field * cos_tab + rotate(field) * sine_tab


def undo_rope(field, cos_tab, sine_tab):
    return field * cos_tab + rotate_back(field * sine_tab)


def norm_back(layer_in, row_inverse_scale, norm_weight, normalized_gradient):
    standardized_gradient = normalized_gradient * norm_weight
    standardized_rows = layer_in * row_inverse_scale
    layer_gradient = row_inverse_scale * (
        standardized_gradient
        - standardized_rows
        * jnp.mean(standardized_gradient * standardized_rows, axis=1, keepdims=True)
    )
    return (layer_gradient, jnp.sum(normalized_gradient * standardized_rows, axis=0))


def line_gather(shard, axis, size):
    if size == 1:
        return shard
    rows = shard.shape[0]
    me = lax.axis_index(axis)
    up = [(k, k + 1) for k in range(size - 1)]
    down = [(k + 1, k) for k in range(size - 1)]
    from_low, from_high = [shard], [shard]
    for step in range(1, size):
        from_low.append(lax.ppermute(from_low[-1], axis, up[step - 1 :]))
        from_high.append(lax.ppermute(from_high[-1], axis, down[: size - step]))
    whole = jnp.zeros((size * rows,) + shard.shape[1:], shard.dtype)
    whole = lax.dynamic_update_slice_in_dim(whole, shard, me * rows, 0)
    for slot in range(1, size):
        piece = jnp.where(me + slot < size, from_high[slot], from_low[size - slot])
        whole = lax.dynamic_update_slice_in_dim(
            whole, piece, lax.rem(me + slot, size) * rows, 0
        )
    return whole


def line_scatter(partial, axis, size):
    rows = partial.shape[0] // size
    me = lax.axis_index(axis)

    def rows_of(owner):
        start = jnp.clip(owner, 0, size - 1) * rows
        return lax.dynamic_slice_in_dim(partial, start, rows, 0).astype(F32)

    if size == 1:
        return partial.astype(F32)
    low = high = None
    for step in range(1, size):
        rise, fall = rows_of(me + size - step), rows_of(me - size + step)
        if step > 1:
            rise = rise + low.astype(F32)
            fall = fall + high.astype(F32)
        up = [(k, k + 1) for k in range(step)]
        down = [(k, k - 1) for k in range(size - step, size)]
        low = lax.ppermute(rise.astype(BF16), axis, up)
        high = lax.ppermute(fall.astype(BF16), axis, down)
    return rows_of(me) + low.astype(F32) + high.astype(F32)


def shards(
    tensor_size,
    block_in,
    out_grad,
    segment_ids,
    positions,
    group_token_counts,
    gain_attn,
    w_query,
    w_key,
    w_value,
    w_out,
    gain_mlp,
    w_gate,
    w_up,
    w_down,
):
    tok_rows = block_in.shape[0]
    query_all, key_all, value_all, out_all = (
        lax.all_gather(w_query, "dp", axis=0, tiled=True),
        lax.all_gather(w_key, "dp", axis=0, tiled=True),
        lax.all_gather(w_value, "dp", axis=0, tiled=True),
        lax.all_gather(w_out, "dp", axis=1, tiled=True),
    )
    gate_all, up_all, down_all = (
        lax.all_gather(w_gate, "dp", axis=0, tiled=True),
        lax.all_gather(w_up, "dp", axis=0, tiled=True),
        lax.all_gather(w_down, "dp", axis=1, tiled=True),
    )

    def gather_rows(rows):
        return line_gather(rows, "tensor", tensor_size)

    def scatter_rows(partial):
        return line_scatter(partial, "tensor", tensor_size)

    x_float = block_in.astype(F32)
    attn_scale = lax.rsqrt(jnp.mean(x_float * x_float, axis=1, keepdims=True) + EPSILON)
    attn_normed = (x_float * attn_scale * gain_attn).astype(BF16)
    whole_attn = gather_rows(attn_normed)
    group_rows = whole_attn.shape[0]
    local_heads = query_all.shape[1] // HEAD_DIM
    cos_tab, sine_tab = rope_tables(positions)

    first_live = lax.axis_index("tensor") * tok_rows
    live = (first_live + jnp.arange(tok_rows) < group_token_counts[0]).astype(BF16)
    live_grad = out_grad * live[:, None]
    whole_grad = gather_rows(lax.optimization_barrier((live_grad, whole_attn))[0])

    def split_heads(field):
        return field.reshape(group_rows, local_heads, HEAD_DIM)

    queries = apply_rope(split_heads(matmul(whole_attn, query_all)), cos_tab, sine_tab).astype(
        BF16
    )
    keys_all = apply_rope(split_heads(matmul(whole_attn, key_all)), cos_tab, sine_tab).astype(BF16)
    values = split_heads(matmul(whole_attn, value_all)).astype(BF16)
    block_rows = group_rows // QBLOCKS
    row_order = jnp.arange(group_rows)
    score_scale = HEAD_DIM ** (-0.5)

    def block_scores(block_index):
        low_row = block_index * block_rows
        high_row = low_row + block_rows
        scores = (
            jnp.einsum(
                "qhd,khd->hqk",
                queries[low_row:high_row],
                keys_all[:high_row],
                preferred_element_type=F32,
            )
            * score_scale
        )
        allowed = (segment_ids[low_row:high_row, None] == segment_ids[None, :high_row]) & (
            row_order[None, :high_row] <= row_order[low_row:high_row, None]
        )
        return jnp.where(allowed[None], scores, -1e30)

    attn_parts = []
    total_parts = []
    for block_index in range(QBLOCKS):
        high_row = (block_index + 1) * block_rows
        scores = block_scores(block_index)
        row_max = jnp.max(scores, axis=2, keepdims=True)
        log_total = row_max + jnp.log(jnp.sum(jnp.exp(scores - row_max), axis=2, keepdims=True))
        prob_bf = jnp.exp(scores - log_total).astype(BF16)
        attn_parts.append(
            jnp.einsum(
                "hqk,khd->qhd", prob_bf, values[:high_row], preferred_element_type=F32
            ).astype(BF16)
        )
        total_parts.append(log_total)
    attn_heads = jnp.concatenate(attn_parts, 0)
    attn = attn_heads.reshape(group_rows, local_heads * HEAD_DIM)
    attn_b, whole_grad = lax.optimization_barrier((attn, whole_grad))
    resid = x_float + scatter_rows(matmul(attn_b, out_all))
    mlp_scale = lax.rsqrt(jnp.mean(resid * resid, axis=1, keepdims=True) + EPSILON)
    mlp_normed = (resid * mlp_scale * gain_mlp).astype(BF16)
    whole_mlp = gather_rows(mlp_normed)
    gate_pre = matmul(whole_mlp, gate_all)
    up_pre = matmul(whole_mlp, up_all)
    sigmoid_gate = jax.nn.sigmoid(gate_pre)
    silu_gate = gate_pre * sigmoid_gate
    hidden = (silu_gate * up_pre).astype(BF16)
    d_hidden = right_t(whole_grad, down_all)
    d_gate = (d_hidden * up_pre * sigmoid_gate * (1.0 + gate_pre * (1.0 - sigmoid_gate))).astype(
        BF16
    )
    d_up = (d_hidden * silu_gate).astype(BF16)
    d_norm_mlp = scatter_rows(right_t(d_gate, gate_all) + right_t(d_up, up_all))
    grad_down_part = left_t(hidden, whole_grad).astype(BF16)
    grad_gate_part = left_t(whole_mlp, d_gate).astype(BF16)
    grad_up_part = left_t(whole_mlp, d_up).astype(BF16)
    d_norm_mlp, grad_down_part, grad_gate_part, grad_up_part = lax.optimization_barrier(
        (d_norm_mlp, grad_down_part, grad_gate_part, grad_up_part)
    )
    d_from_mlp, gain_mlp_part = norm_back(resid, mlp_scale, gain_mlp, d_norm_mlp)
    d_resid = live_grad.astype(F32) + d_from_mlp
    d_resid_b = d_resid.astype(BF16)
    whole_resid = gather_rows(d_resid_b)
    hidden, _ = lax.optimization_barrier((hidden, whole_resid))
    down_rows = scatter_rows(matmul(hidden, down_all))
    grad_out_part = left_t(attn, whole_resid)
    d_attn = split_heads(right_t(whole_resid, out_all).astype(BF16))
    d_q_parts = []
    d_key_sum = jnp.zeros((group_rows, local_heads, HEAD_DIM), F32)
    d_value_sum = jnp.zeros((group_rows, local_heads, HEAD_DIM), F32)
    for block_index in range(QBLOCKS):
        low_row = block_index * block_rows
        high_row = low_row + block_rows
        scores = block_scores(block_index)
        prob_full = jnp.exp(scores - total_parts[block_index])
        dout_rows = d_attn[low_row:high_row]
        row_delta = jnp.sum(
            dout_rows.astype(F32) * attn_heads[low_row:high_row].astype(F32), axis=2
        )
        row_delta = jnp.swapaxes(row_delta, 0, 1)[:, :, None]
        d_probs = jnp.einsum(
            "qhd,khd->hqk", dout_rows, values[:high_row], preferred_element_type=F32
        )
        d_scores = (prob_full * (d_probs - row_delta) * score_scale).astype(BF16)
        d_value_sum = d_value_sum.at[:high_row].add(
            jnp.einsum(
                "hqk,qhd->khd", prob_full.astype(BF16), dout_rows, preferred_element_type=F32
            )
        )
        d_q_parts.append(
            jnp.einsum("hqk,khd->qhd", d_scores, keys_all[:high_row], preferred_element_type=F32)
        )
        d_key_sum = d_key_sum.at[:high_row].add(
            jnp.einsum(
                "hqk,qhd->khd", d_scores, queries[low_row:high_row], preferred_element_type=F32
            )
        )
    local_width = local_heads * HEAD_DIM
    d_queries = (
        undo_rope(jnp.concatenate(d_q_parts, 0), cos_tab, sine_tab)
        .astype(BF16)
        .reshape(group_rows, local_width)
    )
    d_keys = undo_rope(d_key_sum, cos_tab, sine_tab).astype(BF16).reshape(group_rows, local_width)
    d_values = d_value_sum.astype(BF16).reshape(group_rows, local_width)
    d_queries, down_rows = lax.optimization_barrier((d_queries, down_rows))
    block_out = (resid + down_rows).astype(BF16)
    d_norm_attn = scatter_rows(
        right_t(d_queries, query_all) + right_t(d_keys, key_all) + right_t(d_values, value_all)
    )
    grad_query_part = left_t(whole_attn, d_queries)
    grad_key_part = left_t(whole_attn, d_keys)
    grad_value_part = left_t(whole_attn, d_values)
    d_from_attn, gain_attn_part = norm_back(x_float, attn_scale, gain_attn, d_norm_attn)
    input_grad = (d_resid + d_from_attn).astype(BF16)

    def sum_groups(partial, dim):
        return lax.psum_scatter(
            partial.astype(BF16), "dp", scatter_dimension=dim, tiled=True
        ).astype(F32)

    grad_down = sum_groups(grad_down_part, 1)
    grad_gate = sum_groups(grad_gate_part, 0)
    grad_up = sum_groups(grad_up_part, 0)
    grad_out = sum_groups(grad_out_part, 1)
    grad_query = sum_groups(grad_query_part, 0)
    grad_key = sum_groups(grad_key_part, 0)
    grad_value = sum_groups(grad_value_part, 0)
    grad_gain_attn, grad_gain_mlp = lax.psum((gain_attn_part, gain_mlp_part), ("dp", "tensor"))
    return (
        block_out,
        input_grad,
        grad_gain_attn,
        grad_query,
        grad_key,
        grad_value,
        grad_out,
        grad_gain_mlp,
        grad_gate,
        grad_up,
        grad_down,
    )


def solution(mesh):
    tensor_size = mesh.shape["tensor"]
    rows = P(("dp", "tensor"), None)
    into, outof = P("dp", "tensor"), P("tensor", "dp")
    return jax.shard_map(
        lambda *args: shards(tensor_size, *args),
        mesh=mesh,
        in_specs=(
            (rows, rows, P("dp"), P("dp"), P("dp"), P())
            + (into, into, into, outof, P(), into, into, outof)
        ),
        out_specs=(rows, rows, P(), into, into, into, outof, P(), into, into, outof),
        check_vma=False,
    )
```

time: 3750 us -> 2130 us (0.57)
  waiting for transfers between devices: 3030 us -> 1130 us
  other arithmetic: 75.1 us -> 214 us
  starting transfers between devices: 0.89 us -> 117 us
    reduce_scatter x11 -> x7, waiting for transfers between devices: 2010 us -> 212 us  [sum_groups(): lax.psum_scatter(partial.astype(BF16), 'dp', scatter_dimension=dim, tiled...]
    ppermute x0 -> x48, waiting for transfers between devices: none -> 913 us  [the longest x12 340 us: line_gather(): from_high.append(lax.ppermute(from_high[-1], axis, down[:size - step]))]
    all_gather x4 -> x0, waiting for transfers between devices: 566 us -> none  [the longest x1 152 us: shards(): whole_mlp = lax.all_gather(mlp_normed, 'tensor', axis=0, tiled=True)]
    all_gather x1, waiting for transfers between devices: 119 us -> 0.01 us  [shards(): lax.all_gather(w_down, 'dp', axis=1, tiled=True)]
    ppermute x0 -> x48, starting transfers between devices: none -> 116 us  [the longest x12 56.7 us: line_scatter(): low = lax.ppermute(rise.astype(BF16), axis, up)]
    all_gather x1, waiting for transfers between devices: 110 us -> 0.01 us  [shards(): lax.all_gather(w_gate, 'dp', axis=0, tiled=True)]
    all_gather x1, waiting for transfers between devices: 88.2 us -> 0.01 us  [shards(): lax.all_gather(w_up, 'dp', axis=0, tiled=True)]
    convert_element_type x7 -> x23, other arithmetic: 19.6 us -> 99 us  [the longest x8 40.5 us: line_scatter(): low = lax.ppermute(rise.astype(BF16), axis, up)]
  transfers between devices with their start and end apart: 22 -> 62, of which waited for: 22 -> 32; matrix products, arithmetic and copies ran while one was open for 10% -> 28% of each run, Pallas kernels for 0% -> 0%
where the time goes in v1:
time: 2130 us; the launch traced here: 2120 us
  waiting for transfers between devices  1130 us (53%)
  matrix products  515 us (24%)
  other arithmetic  214 us (10%)
  starting transfers between devices  117 us (5%)
  local copies, waits for them, and re-layouts  87.7 us (4%)
  blocking collectives  41.2 us (2%)
    ppermute x12, waiting for transfers between devices, line_gather(): from_high.append(lax.ppermute(from_high[-1], axis, down[:size - step]))  340 us
    ppermute x12, waiting for transfers between devices, line_scatter(): low = lax.ppermute(rise.astype(BF16), axis, up)  282 us
    reduce_scatter x7, waiting for transfers between devices, sum_groups(): lax.psum_scatter(partial.astype(BF16), 'dp', scatter_dimension=dim, tiled...  212 us
    dot_general x7, matrix products, right_t(): lax.dot_general(left, right, (((1,), (1,)), ((), ())), preferred_element_...  156 us
    dot_general x7, matrix products, matmul(): return jnp.dot(left, right, preferred_element_type=F32)  155 us
    dot_general x7, matrix products, left_t(): lax.dot_general(left, right, (((0,), (0,)), ((), ())), preferred_element_...  152 us
    ppermute x12, waiting for transfers between devices, line_gather(): from_low.append(lax.ppermute(from_low[-1], axis, up[step - 1:]))  152 us
    ppermute x12, waiting for transfers between devices, line_scatter(): high = lax.ppermute(fall.astype(BF16), axis, down)  139 us
  transfers between devices with their start and end apart: 62, of which 32 were waited for; matrix products, arithmetic and copies ran while one was open for 28% of the time, Pallas kernels for 0%

profile of v1, /device:TPU:0, one launch (start us, length us, event | category | flops | bytes accessed | tf_op | source)
XLA Modules:
  0.0 2121.2 jit_solution(3207090813764504498)
XLA Ops:
  24.6 43.4 %collective-permute-done.1 = bf16[256,4096]{1,0:T(8,128)(2,1)S(1)} collective-permute-done((bf16[256,4096]{1,0:T(8,128)(2,1)S(1)}, bf16[256,4096]{1,0:T(8,128)(2,1)S(1)}, u32[]{:S(2)}, u32[]{:S(2)}) %collective-permute-start.1) | collective-permute-done | bytes 2097184 | tf_op jit(solution)/shard_map/ppermute | solution.py:77
  79.7 43.8 %collective-permute-done.4 = bf16[256,4096]{1,0:T(8,128)(2,1)} collective-permute-done((bf16[256,4096]{1,0:T(8,128)(2,1)}, bf16[256,4096]{1,0:T(8,128)(2,1)}, u32[]{:S(2)}, u32[]{:S(2)}) %collective-permute-start.4) | collective-permute-done | bytes 2097184 | tf_op jit(solution)/shard_map/ppermute | solution.py:78
  132.3 38.9 %collective-permute-done.5 = bf16[256,4096]{1,0:T(8,128)(2,1)S(1)} collective-permute-done((bf16[256,4096]{1,0:T(8,128)(2,1)}, bf16[256,4096]{1,0:T(8,128)(2,1)S(1)}, u32[]{:S(2)}, u32[]{:S(2)}) %collective-permute-start.5) | collective-permute-done | bytes 2097184 | tf_op jit(solution)/shard_map/ppermute | solution.py:78
  177.7 40.0 %collective-permute-done.7 = bf16[256,4096]{1,0:T(8,128)(2,1)} collective-permute-done((bf16[256,4096]{1,0:T(8,128)(2,1)}, bf16[256,4096]{1,0:T(8,128)(2,1)}, u32[]{:S(2)}, u32[]{:S(2)}) %collective-permute-start.7) | collective-permute-done | bytes 2097184 | tf_op jit(solution)/shard_map/ppermute | solution.py:77
  240.5 32.4 %collective-permute-done.10 = bf16[256,4096]{1,0:T(8,128)(2,1)S(1)} collective-permute-done((bf16[256,4096]{1,0:T(8,128)(2,1)}, bf16[256,4096]{1,0:T(8,128)(2,1)S(1)}, u32[]{:S(2)}, u32[]{:S(2)}) %collective-permute-start.10) | collective-permute-done | bytes 2097184 | tf_op jit(solution)/shard_map/ppermute | solution.py:78
  280.3 44.7 %collective-permute-done.11 = bf16[256,4096]{1,0:T(8,128)(2,1)S(1)} collective-permute-done((bf16[256,4096]{1,0:T(8,128)(2,1)S(1)}, bf16[256,4096]{1,0:T(8,128)(2,1)S(1)}, u32[]{:S(2)}, u32[]{:S(2)}) %collective-permute-start.11) | collective-permute-done | bytes 2097184 | tf_op jit(solution)/shard_map/ppermute | solution.py:78
  460.0 37.1 %collective-permute-done.12 = bf16[256,4096]{1,0:T(8,128)(2,1)} collective-permute-done((bf16[256,4096]{1,0:T(8,128)(2,1)}, bf16[256,4096]{1,0:T(8,128)(2,1)}, u32[]{:S(2)}, u32[]{:S(2)}) %collective-permute-start.12) | collective-permute-done | bytes 2097184 | tf_op jit(solution)/shard_map/ppermute | solution.py:107
  507.6 38.4 %collective-permute-done.13 = bf16[256,4096]{1,0:T(8,128)(2,1)} collective-permute-done((bf16[256,4096]{1,0:T(8,128)(2,1)}, bf16[256,4096]{1,0:T(8,128)(2,1)}, u32[]{:S(2)}, u32[]{:S(2)}) %collective-permute-start.13) | collective-permute-done | bytes 2097184 | tf_op jit(solution)/shard_map/ppermute | solution.py:107
  599.1 48.1 %collective-permute-done.17 = bf16[256,4096]{1,0:T(8,128)(2,1)} collective-permute-done((bf16[256,4096]{1,0:T(8,128)(2,1)}, bf16[256,4096]{1,0:T(8,128)(2,1)}, u32[]{:S(2)}, u32[]{:S(2)}) %collective-permute-start.17) | collective-permute-done | bytes 2097184 | tf_op jit(solution)/shard_map/ppermute | solution.py:108
  663.4 36.9 %collective-permute-done.19 = bf16[256,4096]{1,0:T(8,128)(2,1)S(1)} collective-permute-done((bf16[256,4096]{1,0:T(8,128)(2,1)S(1)}, bf16[256,4096]{1,0:T(8,128)(2,1)S(1)}, u32[]{:S(2)}, u32[]{:S(2)}) %collective-permute-start.19) | collective-permute-done | bytes 2097184 | tf_op jit(solution)/shard_map/ppermute | solution.py:77
  709.2 43.7 %collective-permute-done.22 = bf16[256,4096]{1,0:T(8,128)(2,1)S(1)} collective-permute-done((bf16[256,4096]{1,0:T(8,128)(2,1)S(1)}, bf16[256,4096]{1,0:T(8,128)(2,1)S(1)}, u32[]{:S(2)}, u32[]{:S(2)}) %collective-permute-start.22) | collective-permute-done | bytes 2097184 | tf_op jit(solution)/shard_map/ppermute | solution.py:78
  758.9 35.6 %collective-permute-done.23 = bf16[256,4096]{1,0:T(8,128)(2,1)S(1)} collective-permute-done((bf16[256,4096]{1,0:T(8,128)(2,1)S(1)}, bf16[256,4096]{1,0:T(8,128)(2,1)S(1)}, u32[]{:S(2)}, u32[]{:S(2)}) %collective-permute-start.23) | collective-permute-done | bytes 2097184 | tf_op jit(solution)/shard_map/ppermute | solution.py:78
  857.9 37.7 %multiply_convert_fusion = (bf16[1024,2752]{0,1:T(8,128)(2,1)}, bf16[1024,2752]{0,1:T(8,128)(2,1)}, bf16[1024,2752]{0,1:T(8,128)(2,1)}) fusion(f32[1024,2752]{0,1:T(8,128)} %fusion.78, f32[1024,2752]{0,1:T(8,128)} %fusion.77, bf16[1024,4096]{1,0:T(8,128)(2,1)} %select_dynamic-update-slice_fusion.3, bf16[4096,2752]{0,1:T(8,128)(2,1)} %all-gather.18.cloned.1.call-done), kind=kOutput, calls=%fused_computation.4 | convolution fusion | flops 23127719936 | bytes 70385664 | tf_op jit(solution)/shard_map/dot_general | solution.py:15
  926.7 32.1 %convolution_add_fusion = f32[1024,4096]{1,0:T(8,128)S(1)} fusion(f32[1024,4096]{1,0:T(8,128)} %fusion.79, bf16[1024,2752]{0,1:T(8,128)(2,1)} %get-tuple-element.164, bf16[4096,2752]{0,1:T(8,128)(2,1)} %all-gather.18.cloned.1.call-done), kind=kOutput, calls=%fused_computation.13 | convolution fusion | flops 23089643520 | bytes 61734912 | tf_op jit(solution)/shard_map/dot_general | solution.py:23
  963.6 38.3 %collective-permute-done.24 = bf16[256,4096]{1,0:T(8,128)(2,1)S(1)} collective-permute-done((bf16[256,4096]{1,0:T(8,128)(2,1)S(1)}, bf16[256,4096]{1,0:T(8,128)(2,1)S(1)}, u32[]{:S(2)}, u32[]{:S(2)}) %collective-permute-start.24) | collective-permute-done | bytes 2097184 | tf_op jit(solution)/shard_map/ppermute | solution.py:107
  1198.1 43.7 %collective-permute-done.34 = bf16[256,4096]{1,0:T(8,128)(2,1)S(1)} collective-permute-done((bf16[256,4096]{1,0:T(8,128)(2,1)S(1)}, bf16[256,4096]{1,0:T(8,128)(2,1)S(1)}, u32[]{:S(2)}, u32[]{:S(2)}) %collective-permute-start.34) | collective-permute-done | bytes 2097184 | tf_op jit(solution)/shard_map/ppermute | solution.py:78
  1462.7 32.9 %collective-permute-done.37 = bf16[256,4096]{1,0:T(8,128)(2,1)S(1)} collective-permute-done((bf16[256,4096]{1,0:T(8,128)(2,1)S(1)}, bf16[256,4096]{1,0:T(8,128)(2,1)S(1)}, u32[]{:S(2)}, u32[]{:S(2)}) %collective-permute-start.37) | collective-permute-done | bytes 2097184 | tf_op jit(solution)/shard_map/ppermute | solution.py:107
  1540.1 35.5 %collective-permute-done.41 = bf16[256,4096]{1,0:T(8,128)(2,1)} collective-permute-done((bf16[256,4096]{1,0:T(8,128)(2,1)}, bf16[256,4096]{1,0:T(8,128)(2,1)}, u32[]{:S(2)}, u32[]{:S(2)}) %collective-permute-start.41) | collective-permute-done | bytes 2097184 | tf_op jit(solution)/shard_map/ppermute | solution.py:108
  1662.4 37.3 %collective-permute-done.42 = bf16[256,4096]{1,0:T(8,128)(2,1)S(1)} collective-permute-done((bf16[256,4096]{1,0:T(8,128)(2,1)S(1)}, bf16[256,4096]{1,0:T(8,128)(2,1)S(1)}, u32[]{:S(2)}, u32[]{:S(2)}) %collective-permute-start.42) | collective-permute-done | bytes 2097184 | tf_op jit(solution)/shard_map/ppermute | solution.py:107
  1708.5 33.3 %collective-permute-done.43 = bf16[256,4096]{1,0:T(8,128)(2,1)} collective-permute-done((bf16[256,4096]{1,0:T(8,128)(2,1)S(1)}, bf16[256,4096]{1,0:T(8,128)(2,1)}, u32[]{:S(2)}, u32[]{:S(2)}) %collective-permute-start.43) | collective-permute-done | bytes 2097184 | tf_op jit(solution)/shard_map/ppermute | solution.py:107
  1776.5 47.9 %collective-permute-done.47 = bf16[256,4096]{1,0:T(8,128)(2,1)} collective-permute-done((bf16[256,4096]{1,0:T(8,128)(2,1)}, bf16[256,4096]{1,0:T(8,128)(2,1)}, u32[]{:S(2)}, u32[]{:S(2)}) %collective-permute-start.47) | collective-permute-done | bytes 2097184 | tf_op jit(solution)/shard_map/ppermute | solution.py:108
  1832.7 41.2 %all-reduce.2 = (f32[4096]{0:T(1024)}, f32[4096]{0:T(1024)}) all-reduce(f32[4096]{0:T(1024)S(1)} %get-tuple-element.145, f32[4096]{0:T(1024)S(1)} %copy-done.82), channel_id=1, replica_groups=mesh['dp'=8,'tensor'=4] {'dp','tensor'}, use_global_device_ids=true, to_apply=%region_17.18 | all-reduce | flops 8192 | bytes 65536 | tf_op jit(solution)/shard_map/psum | solution.py:297
  1892.5 70.2 %reduce-scatter.18.cloned.1.call-done = bf16[512,2752]{0,1:T(8,128)(2,1)} async-done(((bf16[4096,2752]{0,1:T(8,128)(2,1)}), bf16[512,2752]{0,1:T(8,128)(2,1)}) %reduce-scatter.18.cloned.1.call-update) | async-done | bytes 2818064 | tf_op jit(solution)/shard_map/reduce_scatter | solution.py:286
  1967.7 141.6 %reduce-scatter.20.cloned.1.call-done = bf16[2752,512]{1,0:T(8,128)(2,1)} async-done(((bf16[2752,4096]{1,0:T(8,128)(2,1)}), bf16[2752,512]{1,0:T(8,128)(2,1)}) %reduce-scatter.20.cloned.1.call-update) | async-done | bytes 2818064 | tf_op jit(solution)/shard_map/reduce_scatter | solution.py:286
  (497 shorter events, 1029.7 us)
Async XLA Ops:
  7.2 319.9 %all-gather.8.cloned.1.call-start = ((), (), s32[]{:S(2)}) async-start(), calls=%async_computation.7 | async-start | bytes 9437184 | tf_op jit(solution)/shard_map/all_gather | solution.py:133
  7.9 335.9 %all-gather.10.cloned.1.call-start = ((), (), s32[]{:S(2)}) async-start(), calls=%async_computation.8 | async-start | bytes 9437184 | tf_op jit(solution)/shard_map/all_gather | solution.py:131
  8.7 364.9 %all-gather.12.cloned.1.call-start = ((), (), s32[]{:S(2)}) async-start(), calls=%async_computation.9 | async-start | bytes 9437184 | tf_op jit(solution)/shard_map/all_gather | solution.py:132
  9.4 424.8 %all-gather.14.cloned.1.call-start = ((), (), s32[]{:S(2)}) async-start(), calls=%async_computation.10 | async-start | bytes 9437184 | tf_op jit(solution)/shard_map/all_gather | solution.py:134
  10.0 786.6 %all-gather.20.cloned.1.call-start = ((), (), s32[]{:S(2)}) async-start(), calls=%async_computation.13 | async-start | bytes 25362432 | tf_op jit(solution)/shard_map/all_gather | solution.py:137
  10.6 816.7 %all-gather.16.cloned.1.call-start = ((), (), s32[]{:S(2)}) async-start(), calls=%async_computation.11 | async-start | bytes 25362432 | tf_op jit(solution)/shard_map/all_gather | solution.py:139
  11.1 846.7 %all-gather.18.cloned.1.call-start = ((), (), s32[]{:S(2)}) async-start(), calls=%async_computation.12 | async-start | bytes 25362432 | tf_op jit(solution)/shard_map/all_gather | solution.py:138
  18.3 49.7 %collective-permute-start.1 = (bf16[256,4096]{1,0:T(8,128)(2,1)S(1)}, bf16[256,4096]{1,0:T(8,128)(2,1)S(1)}, u32[]{:S(2)}, u32[]{:S(2)}) collective-permute-start(bf16[256,4096]{1,0:T(8,128)(2,1)S(1)} %get-tuple-element.161), channel_id=1, source_target_pairs={{0,1},{1,2},{2,3},{4,5},{5,6},{6,7},{8,9},{9,10},{10,11},{12,13},{... | collective-permute-start | bytes 6291464 | tf_op jit(solution)/shard_map/ppermute | solution.py:77
  23.3 49.1 %collective-permute-start = (bf16[256,4096]{1,0:T(8,128)(2,1)S(1)}, bf16[256,4096]{1,0:T(8,128)(2,1)}, u32[]{:S(2)}, u32[]{:S(2)}) collective-permute-start(bf16[256,4096]{1,0:T(8,128)(2,1)S(1)} %get-tuple-element.161), channel_id=1, source_target_pairs={{1,0},{2,1},{3,2},{5,4},{6,5},{7,6},{9,8},{10,9},{11,10},{13,12},{... | collective-permute-start | bytes 6291464 | tf_op jit(solution)/shard_map/ppermute | solution.py:78
  72.4 51.0 %collective-permute-start.4 = (bf16[256,4096]{1,0:T(8,128)(2,1)}, bf16[256,4096]{1,0:T(8,128)(2,1)}, u32[]{:S(2)}, u32[]{:S(2)}) collective-permute-start(bf16[256,4096]{1,0:T(8,128)(2,1)} %collective-permute-done), channel_id=1, source_target_pairs={{1,0},{2,1},{5,4},{6,5},{9,8},{10,9},{13,12},{14,13},{17,16},{18,1... | collective-permute-start | bytes 6291464 | tf_op jit(solution)/shard_map/ppermute | solution.py:78
  73.7 51.0 %collective-permute-start.3 = (bf16[256,4096]{1,0:T(8,128)(2,1)}, bf16[256,4096]{1,0:T(8,128)(2,1)}, u32[]{:S(2)}, u32[]{:S(2)}) collective-permute-start(bf16[256,4096]{1,0:T(8,128)(2,1)} %collective-permute-done.2), channel_id=1, source_target_pairs={{2,3},{6,7},{10,11},{14,15},{18,19},{22,23},{26,27},{30,31}} | collective-permute-start | bytes 6291464 | tf_op jit(solution)/shard_map/ppermute | solution.py:77
  219.7 1537.9 %reduce-scatter.10.cloned.1.call-start = ((), (), s32[]{:S(2)}) async-start(), calls=%async_computation.15 | async-start | bytes 9437184 | tf_op jit(solution)/shard_map/reduce_scatter | solution.py:286
  272.9 52.0 %collective-permute-start.11 = (bf16[256,4096]{1,0:T(8,128)(2,1)S(1)}, bf16[256,4096]{1,0:T(8,128)(2,1)S(1)}, u32[]{:S(2)}, u32[]{:S(2)}) collective-permute-start(bf16[256,4096]{1,0:T(8,128)(2,1)S(1)} %collective-permute-done.10), channel_id=1, source_target_pairs={{1,0},{5,4},{9,8},{13,12},{17,16},{21,20},{25,24},{29,28}} | collective-permute-start | bytes 6291464 | tf_op jit(solution)/shard_map/ppermute | solution.py:78
  458.0 49.6 %collective-permute-start.15 = (bf16[256,4096]{1,0:T(8,128)(2,1)}, bf16[256,4096]{1,0:T(8,128)(2,1)}, u32[]{:S(2)}, u32[]{:S(2)}) collective-permute-start(bf16[256,4096]{1,0:T(8,128)(2,1)} %get-tuple-element.180), channel_id=1, source_target_pairs={{3,2},{7,6},{11,10},{15,14},{19,18},{23,22},{27,26},{31,30}} | collective-permute-start | bytes 6291464 | tf_op jit(solution)/shard_map/ppermute | solution.py:108
  566.3 80.9 %collective-permute-start.17 = (bf16[256,4096]{1,0:T(8,128)(2,1)}, bf16[256,4096]{1,0:T(8,128)(2,1)}, u32[]{:S(2)}, u32[]{:S(2)}) collective-permute-start(bf16[256,4096]{1,0:T(8,128)(2,1)} %add_convert_fusion.13), channel_id=1, source_target_pairs={{1,0},{2,1},{3,2},{5,4},{6,5},{7,6},{9,8},{10,9},{11,10},{13,12},{... | collective-permute-start | bytes 6291464 | tf_op jit(solution)/shard_map/ppermute | solution.py:108
  962.8 77.9 %collective-permute-start.27 = (bf16[256,4096]{1,0:T(8,128)(2,1)}, bf16[256,4096]{1,0:T(8,128)(2,1)S(1)}, u32[]{:S(2)}, u32[]{:S(2)}) collective-permute-start(bf16[256,4096]{1,0:T(8,128)(2,1)} %get-tuple-element.176), channel_id=1, source_target_pairs={{3,2},{7,6},{11,10},{15,14},{19,18},{23,22},{27,26},{31,30}} | collective-permute-start | bytes 6291464 | tf_op jit(solution)/shard_map/ppermute | solution.py:108
  1349.0 411.4 %reduce-scatter.12.cloned.1.call-start = ((), (), s32[]{:S(2)}) async-start(), calls=%async_computation.16 | async-start | bytes 9437184 | tf_op jit(solution)/shard_map/reduce_scatter | solution.py:286
  1378.7 384.6 %reduce-scatter.14.cloned.1.call-start = ((), (), s32[]{:S(2)}) async-start(), calls=%async_computation.17 | async-start | bytes 9437184 | tf_op jit(solution)/shard_map/reduce_scatter | solution.py:286
  1433.3 451.3 %reduce-scatter.8.cloned.1.call-start = ((), (), s32[]{:S(2)}) async-start(), calls=%async_computation.14 | async-start | bytes 9437184 | tf_op jit(solution)/shard_map/reduce_scatter | solution.py:286
  1514.1 61.5 %collective-permute-start.41 = (bf16[256,4096]{1,0:T(8,128)(2,1)}, bf16[256,4096]{1,0:T(8,128)(2,1)}, u32[]{:S(2)}, u32[]{:S(2)}) collective-permute-start(bf16[256,4096]{1,0:T(8,128)(2,1)} %add_convert_fusion.5), channel_id=1, source_target_pairs={{1,0},{2,1},{3,2},{5,4},{6,5},{7,6},{9,8},{10,9},{11,10},{13,12},{... | collective-permute-start | bytes 6291464 | tf_op jit(solution)/shard_map/ppermute | solution.py:108
  1596.7 290.7 %reduce-scatter.16.cloned.1.call-start = ((), (), s32[]{:S(2)}) async-start(), calls=%async_computation.18 | async-start | bytes 25362432 | tf_op jit(solution)/shard_map/reduce_scatter | solution.py:286
  1597.2 365.4 %reduce-scatter.18.cloned.1.call-start = ((), (), s32[]{:S(2)}) async-start(), calls=%async_computation.19 | async-start | bytes 25362432 | tf_op jit(solution)/shard_map/reduce_scatter | solution.py:286
  1598.0 511.4 %reduce-scatter.20.cloned.1.call-start = ((), (), s32[]{:S(2)}) async-start(), calls=%async_computation.20 | async-start | bytes 25362432 | tf_op jit(solution)/shard_map/reduce_scatter | solution.py:286
  1756.1 68.4 %collective-permute-start.47 = (bf16[256,4096]{1,0:T(8,128)(2,1)}, bf16[256,4096]{1,0:T(8,128)(2,1)}, u32[]{:S(2)}, u32[]{:S(2)}) collective-permute-start(bf16[256,4096]{1,0:T(8,128)(2,1)} %add_convert_fusion), channel_id=1, source_target_pairs={{1,0},{2,1},{3,2},{5,4},{6,5},{7,6},{9,8},{10,9},{11,10},{13,12},{... | collective-permute-start | bytes 6291464 | tf_op jit(solution)/shard_map/ppermute | solution.py:108
  (151 other events, 3694.5 us)
Sparse Core Ops, SparseCore 0:
  9.9 57.0 all-gather.7
  68.9 54.3 all-gather.9
  125.2 54.3 all-gather.11
  181.4 55.9 all-gather.13
  239.1 118.6 all-gather.19
  359.5 118.6 all-gather.15
  480.1 118.6 all-gather.17
  1349.2 68.3 reduce-scatter.9
  1421.4 71.2 reduce-scatter.11
  1496.0 71.2 reduce-scatter.13
  1596.8 71.1 reduce-scatter.7
  1671.5 143.1 reduce-scatter.15
  1818.9 143.7 reduce-scatter.17
  1966.3 143.0 reduce-scatter.19

commit v2 on v1

v2 whole, which is shorter than its diff:
```python
import jax
import jax.numpy as jnp
import numpy as np
from jax import lax
from jax.experimental import pallas as pl
from jax.experimental.pallas import tpu as pltpu
from jax.sharding import PartitionSpec as P

HEAD_DIM = 128
EPSILON = 1e-05
ROPE_BASE = 10000.0
BF16 = jnp.bfloat16
F32 = jnp.float32
ATTN_ROWS = 256
MASKED = -1e30
STREAMS = 2
TILE = 256


def matmul(left, right):
    return jnp.dot(left, right, preferred_element_type=F32)


def allowed_keys(seg_rows, seg_cols, low, high):
    shape = (high - low, high)
    row = lax.broadcasted_iota(jnp.int32, shape, 0) + low
    col = lax.broadcasted_iota(jnp.int32, shape, 1)
    return (seg_rows[low:high, :] == seg_cols[:, :high]) & (col <= row)


def nt_dot(left, right):
    return lax.dot_general(left, right, (((1,), (1,)), ((), ())), preferred_element_type=F32)


def tn_dot(left, right):
    return lax.dot_general(left, right, (((0,), (0,)), ((), ())), preferred_element_type=F32)


def attn_forward_kernel(qkv_ref, cos_ref, sin_ref, segr_ref, segc_ref, out_ref, kept_ref, lse_ref):
    head = pl.program_id(0)
    rows = qkv_ref.shape[0]
    half = HEAD_DIM // 2
    for part in range(2):
        at = slice(part * HEAD_DIM, (part + 1) * HEAD_DIM)
        raw = qkv_ref[:, at]
        turned = raw * cos_ref[...] + pltpu.roll(raw, half, 1) * sin_ref[...]
        kept_ref[:, at] = turned.astype(BF16)
    kept_ref[:, 2 * HEAD_DIM :] = qkv_ref[:, 2 * HEAD_DIM :].astype(BF16)

    @pl.when(head == 0)
    def _():
        lse_ref[...] = jnp.zeros_like(lse_ref)

    block = min(ATTN_ROWS, rows)
    for low in range(0, rows, block):
        high = low + block
        query = kept_ref[low:high, :HEAD_DIM]
        key = kept_ref[:high, HEAD_DIM : 2 * HEAD_DIM]
        value = kept_ref[:high, 2 * HEAD_DIM :]
        scores = nt_dot(query, key) * HEAD_DIM**-0.5
        scores = jnp.where(allowed_keys(segr_ref, segc_ref, low, high), scores, MASKED)
        top = jnp.max(scores, axis=1, keepdims=True)
        weight = jnp.exp(scores - top)
        total = jnp.sum(weight, axis=1, keepdims=True)
        mixed = jnp.dot(weight.astype(BF16), value, preferred_element_type=F32) / total
        out_ref[low:high, :] = mixed.astype(BF16)
        lane = lax.broadcasted_iota(jnp.int32, (block, HEAD_DIM), 1)
        lse_ref[low:high, :] = jnp.where(lane == head, top + jnp.log(total), lse_ref[low:high, :])


def attn_backward_kernel(
    kept_ref, out_ref, dout_ref, lse_ref, cos_ref, sin_ref, segr_ref, segc_ref, grad_ref, dk_ref, dv_ref
):
    head = pl.program_id(0)
    rows = kept_ref.shape[0]
    half = HEAD_DIM // 2
    scale = HEAD_DIM**-0.5
    block = min(ATTN_ROWS, rows)

    def unturn(grad):
        return grad * cos_ref[...] + pltpu.roll(grad * sin_ref[...], half, 1)

    for low in reversed(range(0, rows, block)):
        high = low + block
        query = kept_ref[low:high, :HEAD_DIM]
        key = kept_ref[:high, HEAD_DIM : 2 * HEAD_DIM]
        value = kept_ref[:high, 2 * HEAD_DIM :]
        dout = dout_ref[low:high, :]
        lane = lax.broadcasted_iota(jnp.int32, (block, HEAD_DIM), 1)
        lse = jnp.sum(jnp.where(lane == head, lse_ref[low:high, :], 0.0), axis=1, keepdims=True)
        delta = jnp.sum(dout.astype(F32) * out_ref[low:high, :].astype(F32), axis=1, keepdims=True)
        scores = nt_dot(query, key) * scale - lse
        scores = jnp.where(allowed_keys(segr_ref, segc_ref, low, high), scores, MASKED)
        prob = jnp.exp(scores)
        d_scores = (prob * (nt_dot(dout, value) - delta) * scale).astype(BF16)
        prob = prob.astype(BF16)
        dq = jnp.dot(d_scores, key, preferred_element_type=F32)
        turn = dq * cos_ref[low:high, :] + pltpu.roll(dq * sin_ref[low:high, :], half, 1)
        grad_ref[low:high, :HEAD_DIM] = turn.astype(BF16)
        dk, dv = tn_dot(d_scores, query), tn_dot(prob, dout)
        if high == rows:
            dk_ref[...] = dk
            dv_ref[...] = dv
        else:
            dk_ref[:high, :] += dk
            dv_ref[:high, :] += dv
    grad_ref[:, HEAD_DIM : 2 * HEAD_DIM] = unturn(dk_ref[...]).astype(BF16)
    grad_ref[:, 2 * HEAD_DIM :] = dv_ref[...].astype(BF16)


def attn_specs(rows):
    one = lambda width: pl.BlockSpec((rows, width), lambda h: (0, h))
    fixed = lambda r, c: pl.BlockSpec((r, c), lambda h: (0, 0))
    tables = [fixed(rows, HEAD_DIM), fixed(rows, HEAD_DIM), fixed(rows, 1), fixed(1, rows)]
    return one, fixed, tables


def attn_forward(qkv, cos, sin, seg):
    rows, width = qkv.shape
    heads = width // (3 * HEAD_DIM)
    one, fixed, tables = attn_specs(rows)
    return pl.pallas_call(
        attn_forward_kernel,
        grid=(heads,),
        in_specs=[one(3 * HEAD_DIM)] + tables,
        out_specs=[one(HEAD_DIM), one(3 * HEAD_DIM), fixed(rows, HEAD_DIM)],
        out_shape=[
            jax.ShapeDtypeStruct((rows, heads * HEAD_DIM), BF16),
            jax.ShapeDtypeStruct((rows, width), BF16),
            jax.ShapeDtypeStruct((rows, HEAD_DIM), F32),
        ],
        **big(),
    )(qkv, cos, sin, seg[:, None], seg[None, :])


def attn_backward(kept, out, dout, lse, cos, sin, seg):
    rows, width = kept.shape
    heads = width // (3 * HEAD_DIM)
    one, fixed, tables = attn_specs(rows)
    return pl.pallas_call(
        attn_backward_kernel,
        grid=(heads,),
        in_specs=[one(3 * HEAD_DIM), one(HEAD_DIM), one(HEAD_DIM), fixed(rows, HEAD_DIM)] + tables,
        out_specs=one(3 * HEAD_DIM),
        out_shape=jax.ShapeDtypeStruct((rows, width), BF16),
        scratch_shapes=[pltpu.VMEM((rows, HEAD_DIM), F32)] * 2,
        **big(),
    )(kept, out, dout, lse, cos, sin, seg[:, None], seg[None, :])


def lanes(width):
    return -(-width // 128) * 128


def weight_grad_kernel(pairs, added, order_ref, *refs):
    lefts, rights, out_ref = refs[:pairs], refs[pairs : 2 * pairs], refs[-1]
    width, room = rights[0].shape[1], out_ref.shape[1]
    total = tn_dot(lefts[0][...], rights[0][...])
    for left, right in zip(lefts[1:], rights[1:]):
        total += tn_dot(left[...], right[...])
    if added:
        total += refs[2 * pairs][:, :width].astype(F32)
    out_ref[:, :width] = total.astype(BF16)
    if room > width:
        out_ref[:, width:] = jnp.zeros((out_ref.shape[0], room - width), BF16)


def weight_grad(lefts, rights, order, depth, added=None):
    width = rights[0].shape[1]
    blocks = order.shape[0]
    rows = sum(left.shape[0] for left in lefts)
    specs = [pl.BlockSpec((left.shape[0], depth), lambda i, o: (0, o[i])) for left in lefts]
    specs += [pl.BlockSpec(right.shape, lambda i, o: (0, 0)) for right in rights]
    extra = []
    if added is not None:
        specs.append(pl.BlockSpec((depth, lanes(width)), lambda i, o: (i, 0)))
        extra = [added]
    return pl.pallas_call(
        lambda *refs: weight_grad_kernel(len(lefts), added is not None, *refs),
        grid_spec=pltpu.PrefetchScalarGridSpec(
            num_scalar_prefetch=1,
            grid=(blocks,),
            in_specs=specs,
            out_specs=pl.BlockSpec((depth, lanes(width)), lambda i, o: (i, 0)),
        ),
        out_shape=jax.ShapeDtypeStruct((blocks * depth, lanes(width)), BF16),
        **big(),
    )(order, *lefts, *rights, *extra)


def pack_kernel(*refs):
    *ins, out_ref = refs
    for part, ref in enumerate(ins):
        out_ref[:, part * HEAD_DIM : (part + 1) * HEAD_DIM] = ref[...]


def pack_heads(weights):
    rows, width = weights[0].shape
    count = len(weights)
    return pl.pallas_call(
        pack_kernel,
        grid=(width // HEAD_DIM,),
        in_specs=[pl.BlockSpec((rows, HEAD_DIM), lambda h: (0, h))] * count,
        out_specs=pl.BlockSpec((rows, count * HEAD_DIM), lambda h: (0, h)),
        out_shape=jax.ShapeDtypeStruct((rows, count * width), BF16),
    )(*weights)


def unpack_kernel(ref, *outs):
    for part, out in enumerate(outs):
        out[...] = ref[:, part * HEAD_DIM : (part + 1) * HEAD_DIM].astype(F32)


def unpack_heads(packed):
    rows, width = packed.shape
    span = 3 * HEAD_DIM
    one = pl.BlockSpec((rows, HEAD_DIM), lambda h: (0, h))
    return pl.pallas_call(
        unpack_kernel,
        grid=(width // span,),
        in_specs=[pl.BlockSpec((rows, span), lambda h: (0, h))],
        out_specs=[one] * 3,
        out_shape=[jax.ShapeDtypeStruct((rows, width // 3), F32)] * 3,
    )(packed)


def big():
    return dict(
        compiler_params=pltpu.CompilerParams(
            dimension_semantics=("arbitrary",), vmem_limit_bytes=56 << 20
        ),
        cost_estimate=pl.CostEstimate(flops=1024, bytes_accessed=1024, transcendentals=0),
    )


def mlp_forward_kernel(rows_ref, gate_ref, up_ref, hidden_ref, gate_out, up_out):
    rows = rows_ref[...]
    gate = jnp.dot(rows, gate_ref[...], preferred_element_type=F32)
    up = jnp.dot(rows, up_ref[...], preferred_element_type=F32)
    hidden_ref[...] = (gate * jax.nn.sigmoid(gate) * up).astype(BF16)
    gate_out[...] = gate
    up_out[...] = up


def mlp_forward(rows, gate, up):
    count, depth = rows.shape
    width = gate.shape[1]
    tile = pl.BlockSpec((count, TILE), lambda i: (0, i))
    weight = pl.BlockSpec((depth, TILE), lambda i: (0, i))
    return pl.pallas_call(
        mlp_forward_kernel,
        grid=(pl.cdiv(width, TILE),),
        in_specs=[pl.BlockSpec((count, depth), lambda i: (0, 0)), weight, weight],
        out_specs=[tile] * 3,
        out_shape=[jax.ShapeDtypeStruct((count, width), kind) for kind in (BF16, F32, F32)],
        **big(),
    )(rows, gate, up)


def mlp_backward_kernel(rows_ref, down_ref, gate_ref, up_ref, d_gate_ref, d_up_ref):
    d_hidden = nt_dot(rows_ref[...], down_ref[...])
    gate, up = gate_ref[...], up_ref[...]
    open_gate = jax.nn.sigmoid(gate)
    d_gate_ref[...] = (d_hidden * up * open_gate * (1.0 + gate * (1.0 - open_gate))).astype(BF16)
    d_up_ref[...] = (d_hidden * (gate * open_gate)).astype(BF16)


def mlp_backward(rows, down, gate, up):
    count, depth = rows.shape
    width = down.shape[0]
    tile = pl.BlockSpec((count, TILE), lambda i: (0, i))
    return pl.pallas_call(
        mlp_backward_kernel,
        grid=(pl.cdiv(width, TILE),),
        in_specs=[
            pl.BlockSpec((count, depth), lambda i: (0, 0)),
            pl.BlockSpec((TILE, depth), lambda i: (i, 0)),
            tile,
            tile,
        ],
        out_specs=[tile] * 2,
        out_shape=[jax.ShapeDtypeStruct((count, width), BF16)] * 2,
        **big(),
    )(rows, down, gate, up)


def pair_kernel(first_ref, second_ref, left_ref, right_ref, out_ref):
    total = nt_dot(first_ref[...], left_ref[...]) + nt_dot(second_ref[...], right_ref[...])
    out_ref[...] = total.astype(out_ref.dtype)


def pair_product(first, second, left, right):
    count, depth = first.shape
    width = left.shape[0]
    whole = pl.BlockSpec((count, depth), lambda i: (0, 0))
    weight = pl.BlockSpec((TILE, depth), lambda i: (i, 0))
    return pl.pallas_call(
        pair_kernel,
        grid=(width // TILE,),
        in_specs=[whole, whole, weight, weight],
        out_specs=pl.BlockSpec((count, TILE), lambda i: (0, i)),
        out_shape=jax.ShapeDtypeStruct((count, width), BF16),
        **big(),
    )(first, second, left, right)


def rope_tables(position):
    half_dim = HEAD_DIM // 2
    freq_index = jnp.arange(half_dim).astype(F32)
    frequency = ROPE_BASE ** (-2.0 * freq_index / HEAD_DIM)
    angles = position.astype(F32)[:, None] * frequency[None, :]
    cos, sin = jnp.cos(angles), jnp.sin(angles)
    return jnp.concatenate([cos, cos], 1), jnp.concatenate([-sin, sin], 1)


def norm_back(layer_in, row_inverse_scale, norm_weight, normalized_gradient):
    standardized_gradient = normalized_gradient * norm_weight
    standardized_rows = layer_in * row_inverse_scale
    layer_gradient = row_inverse_scale * (
        standardized_gradient
        - standardized_rows
        * jnp.mean(standardized_gradient * standardized_rows, axis=1, keepdims=True)
    )
    return (layer_gradient, jnp.sum(normalized_gradient * standardized_rows, axis=0))


def after(value, *earlier):
    return lax.optimization_barrier((value,) + earlier)[0]


class Line:
    def __init__(self, axis, size):
        self.axis, self.size = axis, size
        self.me = lax.axis_index(axis)

    def in_order(self, slots):
        rows = slots[0].shape[0]
        whole = jnp.zeros((self.size * rows,) + slots[0].shape[1:], slots[0].dtype)
        for slot, piece in enumerate(slots):
            whole = lax.dynamic_update_slice_in_dim(
                whole, piece, lax.rem(self.me + slot, self.size) * rows, 0
            )
        return whole

    def slots_of(self, whole):
        rows = whole.shape[0] // self.size
        return [
            lax.dynamic_slice_in_dim(whole, lax.rem(self.me + slot, self.size) * rows, rows, 0)
            for slot in range(self.size)
        ]


class Order:
    def __init__(self):
        self.last = ()

    def after(self, *values):
        held = lax.optimization_barrier(tuple(values) + self.last)[: len(values)]
        return held[0] if len(values) == 1 else held

    def mark(self, *values):
        self.last = tuple(values)
        return values[0] if len(values) == 1 else values

    def pin(self, *values):
        held = lax.optimization_barrier(tuple(values) + self.last)[: len(values)]
        return self.mark(*held)


class Ring:
    def __init__(self, line, order, first):
        self.line, self.order, self.taken, self.came = line, order, 0, ()
        self.first = first

    def take(self):
        if self.came:
            self.came = self.order.pin(*self.came)

    def step(self):
        if self.taken < self.line.size - 1:
            self.take()
            self.taken += 1
            self.send(self.taken)
        return self

    def finish(self):
        while self.taken < self.line.size - 1:
            self.step()
        self.take()
        return self.result()


class Gather(Ring):
    def __init__(self, line, order, shard):
        super().__init__(line, order, shard)
        self.low, self.high = [shard], [shard]

    def send(self, step):
        size, axis = self.line.size, self.line.axis
        if self.came:
            self.low[-1], self.high[-1] = self.came
        up = [(k, k + 1) for k in range(step - 1, size - 1)]
        down = [(k + 1, k) for k in range(size - step)]
        self.came = (lax.ppermute(self.low[-1], axis, up), lax.ppermute(self.high[-1], axis, down))
        self.low.append(self.came[0])
        self.high.append(self.came[1])

    def result(self):
        if self.came:
            self.low[-1], self.high[-1] = self.came
        line = self.line
        slots = [self.first]
        for slot in range(1, line.size):
            near = line.me + slot < line.size
            slots.append(jnp.where(near, self.high[slot], self.low[line.size - slot]))
        return slots


class Scatter(Ring):
    def send(self, step):
        size, axis = self.line.size, self.line.axis
        rise, fall = self.first[size - step].astype(F32), self.first[step].astype(F32)
        if self.came:
            rise = rise + self.came[0].astype(F32)
            fall = fall + self.came[1].astype(F32)
        rise, fall = self.order.pin(rise.astype(BF16), fall.astype(BF16))
        low = lax.ppermute(rise, axis, [(k, k + 1) for k in range(step)])
        high = lax.ppermute(fall, axis, [(k, k - 1) for k in range(size - step, size)])
        self.came = (low, high)

    def result(self):
        total = self.first[0].astype(F32)
        for part in self.came:
            total = total + part.astype(F32)
        return total


def rows_of(whole, count):
    rows = whole.shape[0] // count
    return [whole[k * rows : (k + 1) * rows] for k in range(count)]


class Groups:
    def __init__(self, size, order):
        self.size, self.sequence = size, order
        self.chips = size // 2
        self.core = lax.rem(lax.axis_index("dp"), 2)

    def gradient(self, lefts, rights, core, came):
        lefts = list(lefts)
        lefts[0] = self.sequence.after(lefts[0])
        depth = lefts[0].shape[1] // self.size
        blocks = jnp.arange(self.chips, dtype=jnp.int32) * 2 + core
        return self.sequence.mark(weight_grad(lefts, rights, blocks, depth, came))

    def theirs(self, lefts, rights):
        return self.gradient(lefts, rights, 1 - self.core, None)

    def send(self, theirs):
        theirs = self.sequence.after(theirs)
        return lax.ppermute(theirs, "dp", [(k, k ^ 1) for k in range(self.size)])

    def mine(self, lefts, rights, came):
        return self.gradient(lefts, rights, self.core, came)

    def scatter(self, mine):
        mine = self.sequence.after(mine)
        groups = [[2 * chip + core for chip in range(self.chips)] for core in range(2)]
        return lax.psum_scatter(
            mine, "dp", scatter_dimension=0, tiled=True, axis_index_groups=groups
        )


class Total:
    def __init__(self, value, sizes, order):
        self.value, self.order, self.came = value, order, None
        self.rounds = [
            (axis, size, 1 << bit) for axis, size in sizes for bit in range(size.bit_length() - 1)
        ]
        self.step()

    def step(self):
        if self.came is not None:
            self.value = self.order.mark(self.value + self.order.pin(self.came))
            self.came = None
        if self.rounds:
            axis, size, mask = self.rounds.pop(0)
            self.came = lax.ppermute(self.value, axis, [(k, k ^ mask) for k in range(size)])

    def finish(self):
        while self.came is not None:
            self.step()
        return self.value


def shards(
    sizes,
    block_in,
    out_grad,
    segment_ids,
    positions,
    group_token_counts,
    gain_attn,
    w_query,
    w_key,
    w_value,
    w_out,
    gain_mlp,
    w_gate,
    w_up,
    w_down,
):
    order = Order()
    line = Line("tensor", sizes["tensor"])
    groups = Groups(sizes["dp"], order)
    tok_rows, width = block_in.shape
    streams = range(STREAMS)

    qkv_all = lax.all_gather(pack_heads([w_query, w_key, w_value]), "dp", axis=0, tiled=True)
    out_all = lax.all_gather(w_out, "dp", axis=1, tiled=True)
    gate_all = lax.all_gather(w_gate, "dp", axis=0, tiled=True)
    up_all = lax.all_gather(w_up, "dp", axis=0, tiled=True)

    def timed(fn, first, *rest):
        return order.mark(fn(order.after(first), *rest))

    with jax.named_scope("normed_rows"):
        x_float = block_in.astype(F32)
        attn_scale = lax.rsqrt(jnp.mean(x_float * x_float, axis=1, keepdims=True) + EPSILON)
        attn_normed = order.mark((x_float * attn_scale * gain_attn).astype(BF16))
        ring = Gather(line, order, attn_normed).step()
        whole_attn = order.mark(line.in_order(ring.finish()))
    cos, sin = rope_tables(positions)

    with jax.named_scope("live_rows"):
        first_live = lax.axis_index("tensor") * tok_rows
        live = (first_live + jnp.arange(tok_rows) < group_token_counts[0]).astype(BF16)
        live_grad = out_grad * live[:, None]
        live_ring = Gather(line, order, order.after(live_grad)).step()

    with jax.named_scope("attention"):
        qkv = timed(matmul, whole_attn, qkv_all)
        live_ring.step()
        attn, kept, lse = attn_forward(order.after(qkv), cos, sin, segment_ids)
        order.mark(attn)

    attn_slots = line.slots_of(attn)
    attn_of = [
        jnp.concatenate([rows_of(slot, STREAMS)[k] for slot in attn_slots], 0) for k in streams
    ]
    x_of = rows_of(x_float, STREAMS)

    def result(grad, width):
        return order.mark(order.after(grad).astype(F32)[:, :width])

    def row_scale(rows):
        return lax.rsqrt(jnp.mean(rows * rows, axis=1, keepdims=True) + EPSILON)

    resid, mlp_scale, whole_mlp = [], [], []

    def mlp_rows(k, total):
        resid.append(x_of[k] + total)
        mlp_scale.append(row_scale(resid[k]))
        return order.mark((resid[k] * mlp_scale[k] * gain_mlp).astype(BF16))

    with jax.named_scope("resid"):
        parts = [timed(matmul, attn_of[k], out_all) for k in streams]
        live_ring.step()
        ring = Scatter(line, order, rows_of(parts[0], line.size)).step()
        ring.step()
        live_slots = live_ring.finish()
        live_of = [
            jnp.concatenate([rows_of(slot, STREAMS)[k] for slot in live_slots], 0) for k in streams
        ]
        ring.step()
        gate_all = order.pin(gate_all)
        down_all = lax.all_gather(order.after(w_down), "dp", axis=1, tiled=True)
        total = ring.finish()

    with jax.named_scope("mlp_rows"):
        ring = Gather(line, order, mlp_rows(0, total)).step()
        ring.step()
        later = Scatter(line, order, rows_of(parts[1], line.size)).step()
        ring.step()
        later.step()
        whole_mlp.append(jnp.concatenate(ring.finish(), 0))
        later.step()

    hidden, acts, d_gate, d_up, d_sums = [], [], [], [], []

    def forward(k):
        made = order.mark(*mlp_forward(order.after(whole_mlp[k]), gate_all, up_all))
        hidden.append(made[0])
        acts.append(made[1:])

    def backward(k):
        made = order.mark(*mlp_backward(order.after(live_of[k]), down_all, *acts[k]))
        d_gate.append(made[0])
        d_up.append(made[1])

    def scatter_input(k):
        part = timed(pair_product, d_gate[k], d_up[k], gate_all, up_all)
        return Scatter(line, order, rows_of(part, line.size)).step()

    d_resid, gains_mlp, whole_resid = [], [], []
    live_parts = rows_of(live_grad, STREAMS)

    def gather_residual(k):
        back, gain_part = norm_back(resid[k], mlp_scale[k], gain_mlp, d_sums[k])
        gains_mlp.append(gain_part)
        d_resid.append(live_parts[k].astype(F32) + back)
        return Gather(line, order, order.mark(d_resid[k].astype(BF16))).step()

    with jax.named_scope("mlp"):
        forward(0)
        ring = Gather(line, order, mlp_rows(1, later.finish())).step()
        ring.step()
        ring.step()
        whole_mlp.append(jnp.concatenate(ring.finish(), 0))
        forward(1)
        backward(0)
        early = scatter_input(0)
        theirs = groups.theirs(live_of, hidden)
        early.step()
        down_came = groups.send(theirs)
        backward(1)
        early.step()
        part = timed(pair_product, d_gate[1], d_up[1], gate_all, up_all)

    with jax.named_scope("grads_mlp"):
        d_sums.append(early.finish())
        ring = gather_residual(0)
        down_mine = groups.mine(live_of, hidden, down_came)
        theirs = groups.theirs(whole_mlp, d_gate)
        ring.step()
        later = Scatter(line, order, rows_of(part, line.size)).step()
        grad_down = groups.scatter(down_mine)
        gate_came = groups.send(theirs)
        hidden_slots = [rows_of(hidden[k], line.size) for k in streams]
        hidden_rows = jnp.concatenate([part for slot in zip(*hidden_slots) for part in slot], 0)
        down_part = timed(matmul, hidden_rows, down_all)
        ring.step()
        later.step()
        gate_mine = groups.mine(whole_mlp, d_gate, gate_came)
        whole_resid.append(jnp.concatenate(ring.finish(), 0))
        later.step()
        theirs = groups.theirs(whole_mlp, d_up)
        d_sums.append(later.finish())
        ring = gather_residual(1)
        up_came = groups.send(theirs)
        d_attn_of = [timed(nt_dot, whole_resid[0], out_all).astype(BF16)]
        grad_down = order.pin(grad_down)
        grad_gate = groups.scatter(gate_mine)
        ring.step()
        down_ring = Scatter(line, order, rows_of(down_part, line.size)).step()
        up_mine = groups.mine(whole_mlp, d_up, up_came)
        ring.step()
        whole_resid.append(jnp.concatenate(ring.finish(), 0))
        down_ring.step()

    with jax.named_scope("d_attn"):
        d_attn_of.append(timed(nt_dot, whole_resid[1], out_all).astype(BF16))
        d_attn = line.in_order(
            [
                jnp.concatenate(slot, 0)
                for slot in zip(*[rows_of(d_attn_of[k], line.size) for k in streams])
            ]
        )
        order.mark(d_attn)
        grad_gate = order.pin(grad_gate)
        grad_up = groups.scatter(up_mine)
        d_attn = order.after(d_attn)
        d_qkv = order.mark(attn_backward(kept, attn, d_attn, lse, cos, sin, segment_ids))
        down_ring.step()

    with jax.named_scope("grads_attn"):
        qkv_theirs = groups.theirs([whole_attn], [d_qkv])
        qkv_came = groups.send(qkv_theirs)
        out_theirs = groups.theirs(whole_resid, attn_of)
        qkv_mine = groups.mine([whole_attn], [d_qkv], qkv_came)

    with jax.named_scope("d_norm_attn"):
        grad_up = order.pin(grad_up)
        grad_qkv = groups.scatter(qkv_mine)
        d_norm_part = timed(nt_dot, d_qkv, qkv_all)
        down_sum = down_ring.finish()
        ring = Scatter(line, order, line.slots_of(d_norm_part)).step()

    with jax.named_scope("grads_attn"):
        gain_attn_part = order.mark(
            jnp.sum(order.after(d_norm_part) * whole_attn.astype(F32), axis=0) / gain_attn
        )
        everywhere = (("dp", sizes["dp"]), ("tensor", sizes["tensor"]))
        gains = Total(jnp.stack([gain_attn_part, sum(gains_mlp)]), everywhere, order)
        out_came = groups.send(out_theirs)
        grad_down = result(grad_down, w_down.shape[0]).T
        ring.step()
        gains.step()
        out_mine = groups.mine(whole_resid, attn_of, out_came)
        grad_qkv = order.pin(grad_qkv)
        grad_out = groups.scatter(out_mine)
        gains.step()
        grad_gate = result(grad_gate, w_gate.shape[1])
        ring.step()
        gains.step()
        grad_up = result(grad_up, w_up.shape[1])
        gains.step()
        d_norm_attn = ring.finish()

    with jax.named_scope("input_grad"):
        d_from_attn, _ = norm_back(x_float, attn_scale, gain_attn, d_norm_attn)
        input_grad = order.mark((jnp.concatenate(d_resid, 0) + d_from_attn).astype(BF16))
    with jax.named_scope("gains"):
        grad_gains = gains.finish()
        grad_gain_attn, grad_gain_mlp = grad_gains[0], grad_gains[1]

    with jax.named_scope("results"):
        block_out = (jnp.concatenate(resid, 0) + down_sum).astype(BF16)
        grad_query, grad_key, grad_value = unpack_heads(grad_qkv)
        grad_out = grad_out.astype(F32)
    return (
        block_out,
        input_grad,
        grad_gain_attn,
        grad_query,
        grad_key,
        grad_value,
        grad_out.T,
        grad_gain_mlp,
        grad_gate,
        grad_up,
        grad_down,
    )


def solution(mesh):
    sizes = {axis: mesh.shape[axis] for axis in ("dp", "tensor")}
    rows = P(("dp", "tensor"), None)
    into, outof = P("dp", "tensor"), P("tensor", "dp")
    return jax.shard_map(
        lambda *args: shards(sizes, *args),
        mesh=mesh,
        in_specs=(
            (rows, rows, P("dp"), P("dp"), P("dp"), P())
            + (into, into, into, outof, P(), into, into, outof)
        ),
        out_specs=(rows, rows, P(), into, into, into, outof, P(), into, into, outof),
        check_vma=False,
    )
```

time: 2130 us -> 1440 us (0.68)
  waiting for transfers between devices: 1130 us -> 482 us
  Pallas kernels: 0 us -> 409 us
  matrix products: 515 us -> 124 us
  other arithmetic: 214 us -> 140 us
  starting transfers between devices: 117 us -> 176 us
  blocking collectives: 41.2 us -> 0 us
    ppermute x48 -> x82, waiting for transfers between devices: 913 us -> 477 us  [the longest x18 232 us: send(): lax.ppermute(self.high[-1], axis, down)]
    pallas_call x0 -> x20, Pallas kernels: none -> 409 us  [the longest x10 173 us: weight_grad(): pl.pallas_call(lambda *refs: weight_grad_kernel(len(lefts), added is not...]
    dot_general x38 -> x3, matrix products: 360 us -> 47 us  [nt_dot(): lax.dot_general(left, right, (((1,), (1,)), ((), ())), preferred_element_...]
    reduce_scatter x7 -> x5, waiting for transfers between devices: 212 us -> 3.51 us  [scatter(): lax.psum_scatter(mine, 'dp', scatter_dimension=0, tiled=True, axis_index_...]
    dot_general x7 -> x4, matrix products: 155 us -> 77.2 us  [matmul(): return jnp.dot(left, right, preferred_element_type=F32)]
    ppermute x48 -> x82, starting transfers between devices: 116 us -> 175 us  [the longest x18 80.5 us: send(): low = lax.ppermute(rise, axis, [(k, k + 1) for k in range(step)])]
    convert_element_type x23 -> x18, other arithmetic: 109 us -> 59 us  [the longest x12 41.8 us: send(): rise, fall = self.order.pin(rise.astype(BF16), fall.astype(BF16))]
    psum x1 -> x0, blocking collectives: 41.2 us -> none  [shards(): lax.psum((gain_attn_part, gain_mlp_part), ('dp', 'tensor'))]
  transfers between devices with their start and end apart: 62 -> 92, of which waited for: 32 -> 33; matrix products, arithmetic and copies ran while one was open for 28% -> 22% of each run, Pallas kernels for 0% -> 24%
where the time goes in v2:
time: 1440 us; the launch traced here: 1420 us
  waiting for transfers between devices  482 us (33%)
  Pallas kernels  409 us (28%)
  starting transfers between devices  176 us (12%)
  other arithmetic  140 us (10%)
  matrix products  124 us (9%)
  local copies, waits for them, and re-layouts  77.3 us (5%)
  between operations  16.8 us (1%)
    ppermute x18, waiting for transfers between devices, send(): lax.ppermute(self.high[-1], axis, down)  232 us
    pallas_call x10, Pallas kernels, weight_grad(): pl.pallas_call(lambda *refs: weight_grad_kernel(len(lefts), added is not...  173 us
    ppermute x18, waiting for transfers between devices, send(): low = lax.ppermute(rise, axis, [(k, k + 1) for k in range(step)])  132 us
    ppermute x18, waiting for transfers between devices, send(): lax.ppermute(self.low[-1], axis, up)  88 us
    ppermute x18, starting transfers between devices, send(): low = lax.ppermute(rise, axis, [(k, k + 1) for k in range(step)])  80.5 us
    dot_general x4, matrix products, matmul(): return jnp.dot(left, right, preferred_element_type=F32)  77.2 us
    pallas_call x2, Pallas kernels, pair_product(): pl.pallas_call(pair_kernel, grid=(width // TILE,), in_specs=[whole, whole...  66.1 us
    pallas_call x2, Pallas kernels, mlp_forward(): pl.pallas_call(mlp_forward_kernel, grid=(pl.cdiv(width, TILE),), in_specs...  64.8 us
  transfers between devices with their start and end apart: 92, of which 33 were waited for; matrix products, arithmetic and copies ran while one was open for 22% of the time, Pallas kernels for 24%

profile of v2, /device:TPU:0, one launch (start us, length us, event | category | flops | bytes accessed | tf_op | source)
XLA Modules:
  0.0 1424.6 jit_solution(14929531913742126494)
XLA Ops:
  39.1 43.3 %collective-permute-done = bf16[256,4096]{1,0:T(8,128)(2,1)S(1)} collective-permute-done((bf16[256,4096]{1,0:T(8,128)(2,1)S(1)}, bf16[256,4096]{1,0:T(8,128)(2,1)S(1)}, u32[]{:S(2)}, u32[]{:S(2)}) %collective-permute-start) | collective-permute-done | bytes 2097184 | tf_op jit(solution)/shard_map/normed_rows/ppermute | solution.py:404
  90.0 49.2 %collective-permute-done.3 = bf16[256,4096]{1,0:T(8,128)(2,1)} collective-permute-done((bf16[256,4096]{1,0:T(8,128)(2,1)S(1)}, bf16[256,4096]{1,0:T(8,128)(2,1)}, u32[]{:S(2)}, u32[]{:S(2)}) %collective-permute-start.3) | collective-permute-done | bytes 2097184 | tf_op jit(solution)/shard_map/normed_rows/ppermute | solution.py:404
  150.2 38.8 %collective-permute-done.5 = bf16[256,4096]{1,0:T(8,128)(2,1)} collective-permute-done((bf16[256,4096]{1,0:T(8,128)(2,1)}, bf16[256,4096]{1,0:T(8,128)(2,1)}, u32[]{:S(2)}, u32[]{:S(2)}) %collective-permute-start.5) | collective-permute-done | bytes 2097184 | tf_op jit(solution)/shard_map/normed_rows/ppermute | solution.py:404
  202.9 33.6 %fusion.33.qkv_ref = f32[1024,3072]{1,0:T(8,128)} fusion(bf16[1024,4096]{1,0:T(8,128)(2,1)} %select_dynamic-update-slice_fusion.refs_1_, bf16[4096,3072]{1,0:T(8,128)(2,1)} %all-gather.6.cloned.1.call-done), kind=kOutput, calls=%fused_computation.151 | convolution fusion | flops 25769803776 | bytes 46137344 | tf_op jit(solution)/shard_map/attention/dot_general | solution.py:21
  251.0 22.7 %attention.1 = (bf16[1024,1024]{1,0:T(8,128)(2,1)}, bf16[1024,3072]{1,0:T(8,128)(2,1)}, f32[1024,128]{1,0:T(8,128)}) custom-call(f32[1024,3072]{1,0:T(8,128)} %fusion.33.qkv_ref, f32[1024,128]{1,0:T(8,128)} %pad_maximum_fusion.8.cos_ref, f32[1024,128]{1,0:T(8,128)} %pad_maximum_fusion.9.sin_ref, s32[1024,1]{1,0:T(8,128)} %copy.31.segr_ref, s32[1,1024]{1,0:T(1,128)} %bitcast.34), custom_call_target="tpu_custom_call" | custom-call | flops 1024 | bytes 1024 | tf_op jit(solution)/shard_map/attention/pallas_call | solution.py:122
  321.4 23.3 %collective-permute-done.15 = bf16[256,4096]{1,0:T(8,128)(2,1)} collective-permute-done((bf16[256,4096]{1,0:T(8,128)(2,1)}, bf16[256,4096]{1,0:T(8,128)(2,1)}, u32[]{:S(2)}, u32[]{:S(2)}) %collective-permute-start.15) | collective-permute-done | bytes 2097184 | tf_op jit(solution)/shard_map/resid/ppermute | solution.py:404
  456.6 32.5 %mlp.7 = (bf16[512,2752]{1,0:T(8,128)(2,1)}, f32[512,2752]{1,0:T(8,128)}, f32[512,2752]{1,0:T(8,128)}) custom-call(bf16[512,4096]{1,0:T(8,128)(2,1)} %pad_maximum_fusion.rows_ref.refs_1_, bf16[4096,2752]{1,0:T(8,128)(2,1)} %all-gather.10.cloned.1.call-done.gate_ref.left_ref, bf16[4096,2752]{1,0:T(8,128)(2,1)} %all-gather.12.cloned.1.call-done.up_ref.right_ref), custom_call_target="tpu_custom_call" | custom-call | flops 1024 | bytes 1024 | tf_op jit(solution)/shard_map/mlp/pallas_call | solution.py:250
  528.5 22.1 %collective-permute-done.33 = bf16[128,4096]{1,0:T(8,128)(2,1)S(1)} collective-permute-done((bf16[128,4096]{1,0:T(8,128)(2,1)S(1)}, bf16[128,4096]{1,0:T(8,128)(2,1)S(1)}, u32[]{:S(2)}, u32[]{:S(2)}) %collective-permute-start.33) | collective-permute-done | bytes 1048608 | tf_op jit(solution)/shard_map/mlp/ppermute | solution.py:404
  570.5 32.3 %mlp.8 = (bf16[512,2752]{1,0:T(8,128)(2,1)}, f32[512,2752]{1,0:T(8,128)}, f32[512,2752]{1,0:T(8,128)}) custom-call(bf16[512,4096]{1,0:T(8,128)(2,1)} %pad_maximum_fusion.1.rows_ref.refs_2_, bf16[4096,2752]{1,0:T(8,128)(2,1)} %all-gather.10.cloned.1.call-done.gate_ref.left_ref, bf16[4096,2752]{1,0:T(8,128)(2,1)} %all-gather.12.cloned.1.call-done.up_ref.right_ref), custom_call_target="tpu_custom_call" | custom-call | flops 1024 | bytes 1024 | tf_op jit(solution)/shard_map/mlp/pallas_call | solution.py:250
  602.9 22.4 %mlp.9 = (bf16[512,2752]{1,0:T(8,128)(2,1)}, bf16[512,2752]{1,0:T(8,128)(2,1)}) custom-call(bf16[512,4096]{1,0:T(8,128)(2,1)} %pad_maximum_fusion.3.rows_ref.refs_1_, bf16[2752,4096]{1,0:T(8,128)(2,1)} %all-gather.14.cloned.1.call-done.down_ref, f32[512,2752]{1,0:T(8,128)} %get-tuple-element.235.gate_ref, f32[512,2752]{1,0:T(8,128)} %get-tuple-element.236.up_ref), custom_call_target="tpu_custom_call" | custom-call | flops 1024 | bytes 1024 | tf_op jit(solution)/shard_map/mlp/pallas_call | solution.py:272
  625.2 33.0 %mlp.10 = bf16[512,4096]{1,0:T(8,128)(2,1)} custom-call(bf16[512,2752]{1,0:T(8,128)(2,1)} %get-tuple-element.253.first_ref.refs_3_, bf16[512,2752]{1,0:T(8,128)(2,1)} %get-tuple-element.252.second_ref.refs_3_, bf16[4096,2752]{1,0:T(8,128)(2,1)} %all-gather.10.cloned.1.call-done.gate_ref.left_ref, ...), custom_call_target="tpu_custom_call" | custom-call | flops 1024 | bytes 1024 | tf_op jit(solution)/shard_map/mlp/pallas_call | solution.py:297
  695.4 22.4 %mlp.12 = (bf16[512,2752]{1,0:T(8,128)(2,1)}, bf16[512,2752]{1,0:T(8,128)(2,1)}) custom-call(bf16[512,4096]{1,0:T(8,128)(2,1)} %pad_maximum_fusion.2.refs_2_.rows_ref, bf16[2752,4096]{1,0:T(8,128)(2,1)} %all-gather.14.cloned.1.call-done.down_ref, f32[512,2752]{1,0:T(8,128)} %get-tuple-element.247.gate_ref, f32[512,2752]{1,0:T(8,128)} %get-tuple-element.248.up_ref), custom_call_target="tpu_custom_call" | custom-call | flops 1024 | bytes 1024 | tf_op jit(solution)/shard_map/mlp/pallas_call | solution.py:272
  726.5 33.1 %mlp.13 = bf16[512,4096]{1,0:T(8,128)(2,1)} custom-call(bf16[512,2752]{1,0:T(8,128)(2,1)} %get-tuple-element.268.first_ref.refs_4_, bf16[512,2752]{1,0:T(8,128)(2,1)} %get-tuple-element.263.second_ref.refs_4_, bf16[4096,2752]{1,0:T(8,128)(2,1)} %all-gather.10.cloned.1.call-done.gate_ref.left_ref, ...), custom_call_target="tpu_custom_call" | custom-call | flops 1024 | bytes 1024 | tf_op jit(solution)/shard_map/mlp/pallas_call | solution.py:297
  826.3 29.3 %fusion.36 = f32[1024,4096]{1,0:T(8,128)} fusion(bf16[1024,2752]{1,0:T(8,128)(2,1)S(1)} %slice_dynamic-update-slice_fusion, bf16[2752,4096]{1,0:T(8,128)(2,1)} %all-gather.14.cloned.1.call-done.down_ref), kind=kOutput, calls=%fused_computation.154 | convolution fusion | flops 23085449216 | bytes 44957696 | tf_op jit(solution)/shard_map/grads_mlp/dot_general | solution.py:21
  942.3 20.8 %collective-permute-done.56 = bf16[128,4096]{1,0:T(8,128)(2,1)} collective-permute-done((bf16[128,4096]{1,0:T(8,128)(2,1)S(1)}, bf16[128,4096]{1,0:T(8,128)(2,1)}, u32[]{:S(2)}, u32[]{:S(2)}) %collective-permute-start.56) | collective-permute-done | bytes 1048608 | tf_op jit(solution)/shard_map/grads_mlp/ppermute | solution.py:404
  984.3 19.6 %grads_mlp.9 = bf16[2048,2816]{1,0:T(8,128)(2,1)} custom-call(s32[4]{0:T(128)} %fusion.14.refs_0_, bf16[512,4096]{1,0:T(8,128)(2,1)} %pad_maximum_fusion.rows_ref.refs_1_, bf16[512,4096]{1,0:T(8,128)(2,1)} %pad_maximum_fusion.1.rows_ref.refs_2_, bf16[512,2752]{1,0:T(8,128)(2,1)} %get-tuple-element.252.second_ref.refs_3_, ...), custom_call_target="tpu_custom_call" | custom-call | flops 1024 | bytes 1024 | tf_op jit(solution)/shard_map/grads_mlp/pallas_call | solution.py:178
  1008.8 21.8 %collective-permute-done.64 = bf16[128,4096]{1,0:T(8,128)(2,1)S(1)} collective-permute-done((bf16[128,4096]{1,0:T(8,128)(2,1)}, bf16[128,4096]{1,0:T(8,128)(2,1)S(1)}, u32[]{:S(2)}, u32[]{:S(2)}) %collective-permute-start.64) | collective-permute-done | bytes 1048608 | tf_op jit(solution)/shard_map/grads_mlp/ppermute | solution.py:404
  1052.4 24.4 %d_attn.1.refs_2_ = bf16[1024,3072]{1,0:T(8,128)(2,1)} custom-call(bf16[1024,3072]{1,0:T(8,128)(2,1)} %get-tuple-element.313.kept_ref, bf16[1024,1024]{1,0:T(8,128)(2,1)} %get-tuple-element.197.out_ref, bf16[1024,1024]{1,0:T(8,128)(2,1)} %copy-done.24, f32[1024,128]{1,0:T(8,128)} %get-tuple-element.318.lse_ref, f32[1024,128]{1,0:T(8,128)} %pad_maximum_fusion.8.cos_ref, ...), custom_call_target="tpu_custom_call" | custom-call | flops 1024 | bytes 1024 | tf_op jit(solution)/shard_map/d_attn/pallas_call | solution.py:140
  1076.8 19.4 %collective-permute-done.65 = bf16[256,4096]{1,0:T(8,128)(2,1)S(1)} collective-permute-done((bf16[256,4096]{1,0:T(8,128)(2,1)}, bf16[256,4096]{1,0:T(8,128)(2,1)S(1)}, u32[]{:S(2)}, u32[]{:S(2)}) %collective-permute-start.65) | collective-permute-done | bytes 2097184 | tf_op jit(solution)/shard_map/grads_mlp/ppermute | solution.py:427
  1102.4 19.6 %grads_attn.4 = bf16[2048,3072]{1,0:T(8,128)(2,1)} custom-call(s32[4]{0:T(128)} %fusion.15.refs_0_, bf16[1024,4096]{1,0:T(8,128)(2,1)} %select_dynamic-update-slice_fusion.refs_1_, bf16[1024,3072]{1,0:T(8,128)(2,1)} %d_attn.1.refs_2_), custom_call_target="tpu_custom_call" | custom-call | flops 1024 | bytes 1024 | tf_op jit(solution)/shard_map/grads_attn/pallas_call | solution.py:178
  1141.4 20.7 %grads_attn.6 = bf16[2048,3072]{1,0:T(8,128)(2,1)} custom-call(s32[4]{0:T(128)} %fusion.14.refs_0_, bf16[1024,4096]{1,0:T(8,128)(2,1)} %select_dynamic-update-slice_fusion.refs_1_, bf16[1024,3072]{1,0:T(8,128)(2,1)} %d_attn.1.refs_2_, bf16[2048,3072]{1,0:T(8,128)(2,1)} %collective-permute-done.69.refs_3_), custom_call_target="tpu_custom_call" | custom-call | flops 1024 | bytes 1024 | tf_op jit(solution)/shard_map/grads_attn/pallas_call | solution.py:178
  1171.2 34.4 %fusion.38 = f32[1024,4096]{1,0:T(8,128)} fusion(bf16[1024,3072]{1,0:T(8,128)(2,1)} %d_attn.1.refs_2_, bf16[4096,3072]{1,0:T(8,128)(2,1)} %all-gather.6.cloned.1.call-done), kind=kOutput, calls=%fused_computation.156 | convolution fusion | flops 25769803776 | bytes 48234496 | tf_op jit(solution)/shard_map/d_norm_attn/dot_general | solution.py:32
  1237.8 44.2 %collective-permute-done.70 = bf16[256,4096]{1,0:T(8,128)(2,1)S(1)} collective-permute-done((bf16[256,4096]{1,0:T(8,128)(2,1)S(1)}, bf16[256,4096]{1,0:T(8,128)(2,1)S(1)}, u32[]{:S(2)}, u32[]{:S(2)}) %collective-permute-start.70) | collective-permute-done | bytes 2097184 | tf_op jit(solution)/shard_map/d_norm_attn/ppermute | solution.py:427
  1313.3 23.7 %collective-permute-done.72 = bf16[256,4096]{1,0:T(8,128)(2,1)} collective-permute-done((bf16[256,4096]{1,0:T(8,128)(2,1)}, bf16[256,4096]{1,0:T(8,128)(2,1)}, u32[]{:S(2)}, u32[]{:S(2)}) %collective-permute-start.72) | collective-permute-done | bytes 2097184 | tf_op jit(solution)/shard_map/grads_attn/ppermute | solution.py:427
  (441 shorter events, 721.2 us)
Async XLA Ops:
  7.2 195.7 %all-gather.6.cloned.1.call-start = ((), (), s32[]{:S(2)}) async-start(), calls=%async_computation.5 | async-start | bytes 28311552 | tf_op jit(solution)/shard_map/all_gather | solution.py:519
  13.7 262.0 %all-gather.8.cloned.1.call-start = ((), (), s32[]{:S(2)}) async-start(), calls=%async_computation.6 | async-start | bytes 9437184 | tf_op jit(solution)/shard_map/all_gather | solution.py:520
  14.4 331.0 %all-gather.10.cloned.1.call-start = ((), (), s32[]{:S(2)}) async-start(), calls=%async_computation.7 | async-start | bytes 25952256 | tf_op jit(solution)/shard_map/all_gather | solution.py:521
  18.4 438.2 %all-gather.12.cloned.1.call-start = ((), (), s32[]{:S(2)}) async-start(), calls=%async_computation.8 | async-start | bytes 25952256 | tf_op jit(solution)/shard_map/all_gather | solution.py:522
  23.1 579.7 %all-gather.14.cloned.1.call-start = ((), (), s32[]{:S(2)}) async-start(), calls=%async_computation.9 | async-start | bytes 25362432 | tf_op jit(solution)/shard_map/resid/all_gather | solution.py:577
  32.6 49.9 %collective-permute-start = (bf16[256,4096]{1,0:T(8,128)(2,1)S(1)}, bf16[256,4096]{1,0:T(8,128)(2,1)S(1)}, u32[]{:S(2)}, u32[]{:S(2)}) collective-permute-start(bf16[256,4096]{1,0:T(8,128)(2,1)S(1)} %get-tuple-element.396), channel_id=1, source_target_pairs={{0,1},{1,2},{2,3},{4,5},{5,6},{6,7},{8,9},{9,10},{10,11},{12,13},{... | collective-permute-start | bytes 6291464 | tf_op jit(solution)/shard_map/normed_rows/ppermute | solution.py:404
  37.8 48.9 %collective-permute-start.1 = (bf16[256,4096]{1,0:T(8,128)(2,1)S(1)}, bf16[256,4096]{1,0:T(8,128)(2,1)S(1)}, u32[]{:S(2)}, u32[]{:S(2)}) collective-permute-start(bf16[256,4096]{1,0:T(8,128)(2,1)S(1)} %get-tuple-element.396), channel_id=1, source_target_pairs={{1,0},{2,1},{3,2},{5,4},{6,5},{7,6},{9,8},{10,9},{11,10},{13,12},{... | collective-permute-start | bytes 6291464 | tf_op jit(solution)/shard_map/normed_rows/ppermute | solution.py:404
  88.7 50.5 %collective-permute-start.3 = (bf16[256,4096]{1,0:T(8,128)(2,1)S(1)}, bf16[256,4096]{1,0:T(8,128)(2,1)}, u32[]{:S(2)}, u32[]{:S(2)}) collective-permute-start(bf16[256,4096]{1,0:T(8,128)(2,1)S(1)} %collective-permute-done.1), channel_id=1, source_target_pairs={{1,0},{2,1},{5,4},{6,5},{9,8},{10,9},{13,12},{14,13},{17,16},{18,1... | collective-permute-start | bytes 6291464 | tf_op jit(solution)/shard_map/normed_rows/ppermute | solution.py:404
  345.4 590.6 %reduce-scatter.6.cloned.1.call-start = ((), (), s32[]{:S(2)}) async-start(), calls=%async_computation.10 | async-start | bytes 14417920 | tf_op jit(solution)/shard_map/grads_mlp/reduce_scatter | solution.py:469
  691.5 82.9 %collective-permute-start.44 = (bf16[2048,2816]{1,0:T(8,128)(2,1)}, bf16[2048,2816]{1,0:T(8,128)(2,1)}, u32[]{:S(2)}, u32[]{:S(2)}) collective-permute-start(bf16[2048,2816]{1,0:T(8,128)(2,1)} %mlp.11), channel_id=1, source_target_pairs={{0,4},{4,0},{8,12},{12,8},{16,20},{20,16},{24,28},{28,24},{1,5},{5... | collective-permute-start | bytes 34603016 | tf_op jit(solution)/shard_map/mlp/ppermute | solution.py:461
  813.1 234.5 %reduce-scatter.8.cloned.1.call-start = ((), (), s32[]{:S(2)}) async-start(), calls=%async_computation.11 | async-start | bytes 14417920 | tf_op jit(solution)/shard_map/grads_mlp/reduce_scatter | solution.py:469
  813.1 57.1 %collective-permute-start.53 = (bf16[2048,2816]{1,0:T(8,128)(2,1)}, bf16[2048,2816]{1,0:T(8,128)(2,1)}, u32[]{:S(2)}, u32[]{:S(2)}) collective-permute-start(bf16[2048,2816]{1,0:T(8,128)(2,1)} %grads_mlp.6), channel_id=1, source_target_pairs={{0,4},{4,0},{8,12},{12,8},{16,20},{20,16},{24,28},{28,24},{1,5},{5... | collective-permute-start | bytes 34603016 | tf_op jit(solution)/shard_map/grads_mlp/ppermute | solution.py:461
  936.0 226.8 %reduce-scatter.10.cloned.1.call-start = ((), (), s32[]{:S(2)}) async-start(), calls=%async_computation.12 | async-start | bytes 14417920 | tf_op jit(solution)/shard_map/d_attn/reduce_scatter | solution.py:469
  977.7 52.9 %collective-permute-start.58 = (bf16[256,4096]{1,0:T(8,128)(2,1)}, bf16[256,4096]{1,0:T(8,128)(2,1)S(1)}, u32[]{:S(2)}, u32[]{:S(2)}) collective-permute-start(bf16[256,4096]{1,0:T(8,128)(2,1)} %get-tuple-element.301), channel_id=1, source_target_pairs={{0,1},{4,5},{8,9},{12,13},{16,17},{20,21},{24,25},{28,29}} | collective-permute-start | bytes 6291464 | tf_op jit(solution)/shard_map/grads_mlp/ppermute | solution.py:427
  1047.6 261.0 %reduce-scatter.12.cloned.1.call-start = ((), (), s32[]{:S(2)}) async-start(), calls=%async_computation.13 | async-start | bytes 15728640 | tf_op jit(solution)/shard_map/d_norm_attn/reduce_scatter | solution.py:469
  1047.6 48.6 %collective-permute-start.65 = (bf16[256,4096]{1,0:T(8,128)(2,1)}, bf16[256,4096]{1,0:T(8,128)(2,1)S(1)}, u32[]{:S(2)}, u32[]{:S(2)}) collective-permute-start(bf16[256,4096]{1,0:T(8,128)(2,1)} %get-tuple-element.311), channel_id=1, source_target_pairs={{0,1},{1,2},{4,5},{5,6},{8,9},{9,10},{12,13},{13,14},{16,17},{17,1... | collective-permute-start | bytes 6291464 | tf_op jit(solution)/shard_map/grads_mlp/ppermute | solution.py:427
  1162.8 251.4 %reduce-scatter.14.cloned.1.call-start = ((), (), s32[]{:S(2)}) async-start(), calls=%async_computation.14 | async-start | bytes 5242880 | tf_op jit(solution)/shard_map/grads_attn/reduce_scatter | solution.py:469
  1162.9 52.1 %collective-permute-start.67 = (bf16[256,4096]{1,0:T(8,128)(2,1)}, bf16[256,4096]{1,0:T(8,128)(2,1)S(1)}, u32[]{:S(2)}, u32[]{:S(2)}) collective-permute-start(bf16[256,4096]{1,0:T(8,128)(2,1)} %get-tuple-element.321), channel_id=1, source_target_pairs={{0,1},{1,2},{2,3},{4,5},{5,6},{6,7},{8,9},{9,10},{10,11},{12,13},{... | collective-permute-start | bytes 6291464 | tf_op jit(solution)/shard_map/d_attn/ppermute | solution.py:427
  1169.7 49.2 %collective-permute-start.68 = (bf16[256,4096]{1,0:T(8,128)(2,1)S(1)}, bf16[256,4096]{1,0:T(8,128)(2,1)S(1)}, u32[]{:S(2)}, u32[]{:S(2)}) collective-permute-start(bf16[256,4096]{1,0:T(8,128)(2,1)S(1)} %get-tuple-element.322), channel_id=1, source_target_pairs={{1,0},{2,1},{3,2},{5,4},{6,5},{7,6},{9,8},{10,9},{11,10},{13,12},{... | collective-permute-start | bytes 6291464 | tf_op jit(solution)/shard_map/d_attn/ppermute | solution.py:428
  1234.5 62.1 %collective-permute-start.76 = (bf16[2048,1024]{1,0:T(8,128)(2,1)S(1)}, bf16[2048,1024]{1,0:T(8,128)(2,1)S(1)}, u32[]{:S(2)}, u32[]{:S(2)}) collective-permute-start(bf16[2048,1024]{1,0:T(8,128)(2,1)S(1)} %copy-done.25), channel_id=1, source_target_pairs={{0,4},{4,0},{8,12},{12,8},{16,20},{20,16},{24,28},{28,24},{1,5},{5... | collective-permute-start | bytes 12582920 | tf_op jit(solution)/shard_map/grads_attn/ppermute | solution.py:461
  1237.5 57.6 %collective-permute-start.74 = (f32[2,4096]{1,0:T(2,128)S(1)}, f32[2,4096]{1,0:T(2,128)S(1)}, u32[]{:S(2)}, u32[]{:S(2)}) collective-permute-start(f32[2,4096]{1,0:T(2,128)S(1)} %pad_maximum_fusion.10), channel_id=1, source_target_pairs={{0,4},{4,0},{8,12},{12,8},{16,20},{20,16},{24,28},{28,24},{1,5},{5... | collective-permute-start | bytes 98312 | tf_op jit(solution)/shard_map/grads_attn/ppermute | solution.py:488
  1287.5 49.5 %collective-permute-start.72 = (bf16[256,4096]{1,0:T(8,128)(2,1)}, bf16[256,4096]{1,0:T(8,128)(2,1)}, u32[]{:S(2)}, u32[]{:S(2)}) collective-permute-start(bf16[256,4096]{1,0:T(8,128)(2,1)} %get-tuple-element.338), channel_id=1, source_target_pairs={{0,1},{1,2},{4,5},{5,6},{8,9},{9,10},{12,13},{13,14},{16,17},{17,1... | collective-permute-start | bytes 6291464 | tf_op jit(solution)/shard_map/grads_attn/ppermute | solution.py:427
  1345.2 57.8 %collective-permute-start.77 = (bf16[256,4096]{1,0:T(8,128)(2,1)}, bf16[256,4096]{1,0:T(8,128)(2,1)}, u32[]{:S(2)}, u32[]{:S(2)}) collective-permute-start(bf16[256,4096]{1,0:T(8,128)(2,1)} %get-tuple-element.349), channel_id=1, source_target_pairs={{0,1},{1,2},{2,3},{4,5},{5,6},{6,7},{8,9},{9,10},{10,11},{12,13},{... | collective-permute-start | bytes 6291464 | tf_op jit(solution)/shard_map/grads_attn/ppermute | solution.py:427
  1354.6 48.5 %collective-permute-start.78 = (bf16[256,4096]{1,0:T(8,128)(2,1)}, bf16[256,4096]{1,0:T(8,128)(2,1)}, u32[]{:S(2)}, u32[]{:S(2)}) collective-permute-start(bf16[256,4096]{1,0:T(8,128)(2,1)} %get-tuple-element.350), channel_id=1, source_target_pairs={{1,0},{2,1},{3,2},{5,4},{6,5},{7,6},{9,8},{10,9},{11,10},{13,12},{... | collective-permute-start | bytes 6291464 | tf_op jit(solution)/shard_map/grads_attn/ppermute | solution.py:428
  (133 other events, 3333.3 us)
Sparse Core Ops, SparseCore 0:
  13.8 128.0 all-gather.5
  143.7 55.9 all-gather.7
  202.2 116.4 all-gather.9
  320.4 116.4 all-gather.11
  438.6 118.6 all-gather.13
  813.2 111.1 reduce-scatter.5
  936.2 111.3 reduce-scatter.7
  1050.7 112.0 reduce-scatter.9
  1165.9 120.7 reduce-scatter.11
  1308.7 51.1 reduce-scatter.13

commit v3 on v2

--- a/solution.py
+++ b/solution.py
@@ -224,6 +224,21 @@
     )(packed)
 
 
+def turned_kernel(in_ref, out_ref):
+    out_ref[...] = in_ref[...].astype(F32).T
+
+
+def turned_result(grad, width):
+    rows = grad.shape[0]
+    return pl.pallas_call(
+        turned_kernel,
+        grid=(pl.cdiv(width, TILE),),
+        in_specs=[pl.BlockSpec((rows, TILE), lambda i: (0, i))],
+        out_specs=pl.BlockSpec((TILE, rows), lambda i: (i, 0)),
+        out_shape=jax.ShapeDtypeStruct((width, rows), F32),
+    )(grad)
+
+
 def big():
     return dict(
         compiler_params=pltpu.CompilerParams(
@@ -550,9 +565,6 @@
     ]
     x_of = rows_of(x_float, STREAMS)
 
-    def result(grad, width):
-        return order.mark(order.after(grad).astype(F32)[:, :width])
-
     def row_scale(rows):
         return lax.rsqrt(jnp.mean(rows * rows, axis=1, keepdims=True) + EPSILON)
 
@@ -614,49 +626,46 @@
     with jax.named_scope("mlp"):
         forward(0)
         ring = Gather(line, order, mlp_rows(1, later.finish())).step()
-        ring.step()
-        ring.step()
         whole_mlp.append(jnp.concatenate(ring.finish(), 0))
-        forward(1)
         backward(0)
         early = scatter_input(0)
+        forward(1)
+        early.step()
         theirs = groups.theirs(live_of, hidden)
         early.step()
         down_came = groups.send(theirs)
         backward(1)
-        early.step()
-        part = timed(pair_product, d_gate[1], d_up[1], gate_all, up_all)
 
     with jax.named_scope("grads_mlp"):
         d_sums.append(early.finish())
         ring = gather_residual(0)
+        part = timed(pair_product, d_gate[1], d_up[1], gate_all, up_all)
+        ring.step()
+        later = Scatter(line, order, rows_of(part, line.size)).step()
         down_mine = groups.mine(live_of, hidden, down_came)
+        ring.step()
+        later.step()
+        grad_down = groups.scatter(down_mine)
         theirs = groups.theirs(whole_mlp, d_gate)
-        ring.step()
-        later = Scatter(line, order, rows_of(part, line.size)).step()
-        grad_down = groups.scatter(down_mine)
-        gate_came = groups.send(theirs)
-        hidden_slots = [rows_of(hidden[k], line.size) for k in streams]
-        hidden_rows = jnp.concatenate([part for slot in zip(*hidden_slots) for part in slot], 0)
-        down_part = timed(matmul, hidden_rows, down_all)
-        ring.step()
-        later.step()
-        gate_mine = groups.mine(whole_mlp, d_gate, gate_came)
         whole_resid.append(jnp.concatenate(ring.finish(), 0))
         later.step()
+        gate_came = groups.send(theirs)
         theirs = groups.theirs(whole_mlp, d_up)
         d_sums.append(later.finish())
         ring = gather_residual(1)
         up_came = groups.send(theirs)
-        d_attn_of = [timed(nt_dot, whole_resid[0], out_all).astype(BF16)]
+        gate_mine = groups.mine(whole_mlp, d_gate, gate_came)
+        ring.step()
         grad_down = order.pin(grad_down)
         grad_gate = groups.scatter(gate_mine)
-        ring.step()
+        up_mine = groups.mine(whole_mlp, d_up, up_came)
+        ring.step()
+        hidden_slots = [rows_of(hidden[k], line.size) for k in streams]
+        hidden_rows = jnp.concatenate([part for slot in zip(*hidden_slots) for part in slot], 0)
+        down_part = timed(matmul, hidden_rows, down_all)
+        d_attn_of = [timed(nt_dot, whole_resid[0], out_all).astype(BF16)]
+        whole_resid.append(jnp.concatenate(ring.finish(), 0))
         down_ring = Scatter(line, order, rows_of(down_part, line.size)).step()
-        up_mine = groups.mine(whole_mlp, d_up, up_came)
-        ring.step()
-        whole_resid.append(jnp.concatenate(ring.finish(), 0))
-        down_ring.step()
 
     with jax.named_scope("d_attn"):
         d_attn_of.append(timed(nt_dot, whole_resid[1], out_all).astype(BF16))
@@ -671,40 +680,42 @@
         grad_up = groups.scatter(up_mine)
         d_attn = order.after(d_attn)
         d_qkv = order.mark(attn_backward(kept, attn, d_attn, lse, cos, sin, segment_ids))
-        down_ring.step()
 
     with jax.named_scope("grads_attn"):
         qkv_theirs = groups.theirs([whole_attn], [d_qkv])
+        down_ring.step()
         qkv_came = groups.send(qkv_theirs)
         out_theirs = groups.theirs(whole_resid, attn_of)
         qkv_mine = groups.mine([whole_attn], [d_qkv], qkv_came)
+        down_ring.step()
 
     with jax.named_scope("d_norm_attn"):
-        grad_up = order.pin(grad_up)
-        grad_qkv = groups.scatter(qkv_mine)
         d_norm_part = timed(nt_dot, d_qkv, qkv_all)
         down_sum = down_ring.finish()
         ring = Scatter(line, order, line.slots_of(d_norm_part)).step()
 
     with jax.named_scope("grads_attn"):
+        grad_up = order.pin(grad_up)
+        grad_qkv = groups.scatter(qkv_mine)
         gain_attn_part = order.mark(
             jnp.sum(order.after(d_norm_part) * whole_attn.astype(F32), axis=0) / gain_attn
         )
         everywhere = (("dp", sizes["dp"]), ("tensor", sizes["tensor"]))
         gains = Total(jnp.stack([gain_attn_part, sum(gains_mlp)]), everywhere, order)
         out_came = groups.send(out_theirs)
-        grad_down = result(grad_down, w_down.shape[0]).T
+        grad_down = timed(turned_result, grad_down, w_down.shape[0])
         ring.step()
         gains.step()
         out_mine = groups.mine(whole_resid, attn_of, out_came)
+        gains.step()
+        grad_gate = timed(turned_result, grad_gate, w_gate.shape[1]).T
+        ring.step()
+        gains.step()
+        grad_up = timed(turned_result, grad_up, w_up.shape[1]).T
+        gains.step()
         grad_qkv = order.pin(grad_qkv)
         grad_out = groups.scatter(out_mine)
-        gains.step()
-        grad_gate = result(grad_gate, w_gate.shape[1])
-        ring.step()
-        gains.step()
-        grad_up = result(grad_up, w_up.shape[1])
-        gains.step()
+        grad_query, grad_key, grad_value = order.mark(*unpack_heads(order.after(grad_qkv)))
         d_norm_attn = ring.finish()
 
     with jax.named_scope("input_grad"):
@@ -716,8 +727,7 @@
 
     with jax.named_scope("results"):
         block_out = (jnp.concatenate(resid, 0) + down_sum).astype(BF16)
-        grad_query, grad_key, grad_value = unpack_heads(grad_qkv)
-        grad_out = grad_out.astype(F32)
+        grad_out = turned_result(grad_out, w_out.shape[0])
     return (
         block_out,
         input_grad,
@@ -725,7 +735,7 @@
         grad_query,
         grad_key,
         grad_value,
-        grad_out.T,
+        grad_out,
         grad_gain_mlp,
         grad_gate,
         grad_up,

time: 1440 us -> 1420 us (0.986)
  waiting for transfers between devices: 482 us -> 451 us
  Pallas kernels: 409 us -> 437 us
  local copies, waits for them, and re-layouts: 77.3 us -> 52.8 us
    pallas_call x0 -> x4, Pallas kernels: none -> 29 us  [turned_result(): pl.pallas_call(turned_kernel, grid=(pl.cdiv(width, TILE),), in_specs=[pl....]
    unnamed x143 -> x129, local copies, waits for them, and re-layouts: 42.9 us -> 18.5 us
    ppermute x18, waiting for transfers between devices: 88 us -> 68.7 us  [send(): lax.ppermute(self.low[-1], axis, up)]
    ppermute x18, waiting for transfers between devices: 232 us -> 215 us  [send(): lax.ppermute(self.high[-1], axis, down)]
    reduce_scatter x5, waiting for transfers between devices: 3.51 us -> 18.1 us  [scatter(): lax.psum_scatter(mine, 'dp', scatter_dimension=0, tiled=True, axis_index_...]
    ppermute x18, waiting for transfers between devices: 8.75 us -> 23.3 us  [send(): lax.ppermute(fall, axis, [(k, k - 1) for k in range(size - step, size)])]
  transfers between devices with their start and end apart: 92 -> 92, of which waited for: 33 -> 40; matrix products, arithmetic and copies ran while one was open for 22% -> 22% of each run, Pallas kernels for 24% -> 26%
where the time goes in v3:
time: 1420 us; the launch traced here: 1400 us
  waiting for transfers between devices  451 us (32%)
  Pallas kernels  437 us (31%)
  starting transfers between devices  175 us (12%)
  other arithmetic  142 us (10%)
  matrix products  131 us (9%)
  local copies, waits for them, and re-layouts  52.8 us (4%)
  between operations  16.7 us (1%)
    ppermute x18, waiting for transfers between devices, send(): lax.ppermute(self.high[-1], axis, down)  215 us
    pallas_call x10, Pallas kernels, weight_grad(): pl.pallas_call(lambda *refs: weight_grad_kernel(len(lefts), added is not...  172 us
    ppermute x18, waiting for transfers between devices, send(): low = lax.ppermute(rise, axis, [(k, k + 1) for k in range(step)])  121 us
    ppermute x18, starting transfers between devices, send(): low = lax.ppermute(rise, axis, [(k, k + 1) for k in range(step)])  78.1 us
    dot_general x4, matrix products, matmul(): return jnp.dot(left, right, preferred_element_type=F32)  77.3 us
    ppermute x18, waiting for transfers between devices, send(): lax.ppermute(self.low[-1], axis, up)  68.7 us
    pallas_call x2, Pallas kernels, pair_product(): pl.pallas_call(pair_kernel, grid=(width // TILE,), in_specs=[whole, whole...  66.1 us
    pallas_call x2, Pallas kernels, mlp_forward(): pl.pallas_call(mlp_forward_kernel, grid=(pl.cdiv(width, TILE),), in_specs...  65 us
  transfers between devices with their start and end apart: 92, of which 40 were waited for; matrix products, arithmetic and copies ran while one was open for 22% of the time, Pallas kernels for 26%

profile of v3, /device:TPU:0, one launch (start us, length us, event | category | flops | bytes accessed | tf_op | source)
XLA Modules:
  0.0 1404.6 jit_solution(11244056763567597924)
XLA Ops:
  39.2 43.3 %collective-permute-done = bf16[256,4096]{1,0:T(8,128)(2,1)S(1)} collective-permute-done((bf16[256,4096]{1,0:T(8,128)(2,1)S(1)}, bf16[256,4096]{1,0:T(8,128)(2,1)S(1)}, u32[]{:S(2)}, u32[]{:S(2)}) %collective-permute-start) | collective-permute-done | bytes 2097184 | tf_op jit(solution)/shard_map/normed_rows/ppermute | solution.py:419
  90.1 49.3 %collective-permute-done.3 = bf16[256,4096]{1,0:T(8,128)(2,1)} collective-permute-done((bf16[256,4096]{1,0:T(8,128)(2,1)S(1)}, bf16[256,4096]{1,0:T(8,128)(2,1)}, u32[]{:S(2)}, u32[]{:S(2)}) %collective-permute-start.3) | collective-permute-done | bytes 2097184 | tf_op jit(solution)/shard_map/normed_rows/ppermute | solution.py:419
  150.3 38.8 %collective-permute-done.5 = bf16[256,4096]{1,0:T(8,128)(2,1)} collective-permute-done((bf16[256,4096]{1,0:T(8,128)(2,1)}, bf16[256,4096]{1,0:T(8,128)(2,1)}, u32[]{:S(2)}, u32[]{:S(2)}) %collective-permute-start.5) | collective-permute-done | bytes 2097184 | tf_op jit(solution)/shard_map/normed_rows/ppermute | solution.py:419
  202.9 33.8 %fusion.32.qkv_ref = f32[1024,3072]{1,0:T(8,128)} fusion(bf16[1024,4096]{1,0:T(8,128)(2,1)} %select_dynamic-update-slice_fusion.refs_1_, bf16[4096,3072]{1,0:T(8,128)(2,1)} %all-gather.6.cloned.1.call-done), kind=kOutput, calls=%fused_computation.146 | convolution fusion | flops 25769803776 | bytes 46137344 | tf_op jit(solution)/shard_map/attention/dot_general | solution.py:21
  251.2 22.7 %attention.1 = (bf16[1024,1024]{1,0:T(8,128)(2,1)}, bf16[1024,3072]{1,0:T(8,128)(2,1)}, f32[1024,128]{1,0:T(8,128)}) custom-call(f32[1024,3072]{1,0:T(8,128)} %fusion.32.qkv_ref, f32[1024,128]{1,0:T(8,128)} %pad_maximum_fusion.8.cos_ref, f32[1024,128]{1,0:T(8,128)} %pad_maximum_fusion.9.sin_ref, s32[1024,1]{1,0:T(8,128)} %copy.27.segr_ref, s32[1,1024]{1,0:T(1,128)} %bitcast.36), custom_call_target="tpu_custom_call" | custom-call | flops 1024 | bytes 1024 | tf_op jit(solution)/shard_map/attention/pallas_call | solution.py:122
  321.6 23.3 %collective-permute-done.15 = bf16[256,4096]{1,0:T(8,128)(2,1)} collective-permute-done((bf16[256,4096]{1,0:T(8,128)(2,1)}, bf16[256,4096]{1,0:T(8,128)(2,1)}, u32[]{:S(2)}, u32[]{:S(2)}) %collective-permute-start.15) | collective-permute-done | bytes 2097184 | tf_op jit(solution)/shard_map/resid/ppermute | solution.py:419
  455.9 32.6 %mlp.6 = (bf16[512,2752]{1,0:T(8,128)(2,1)}, f32[512,2752]{1,0:T(8,128)}, f32[512,2752]{1,0:T(8,128)}) custom-call(bf16[512,4096]{1,0:T(8,128)(2,1)} %pad_maximum_fusion.rows_ref.refs_1_, bf16[4096,2752]{1,0:T(8,128)(2,1)} %all-gather.10.cloned.1.call-done.gate_ref.left_ref, bf16[4096,2752]{1,0:T(8,128)(2,1)} %all-gather.12.cloned.1.call-done.up_ref.right_ref), custom_call_target="tpu_custom_call" | custom-call | flops 1024 | bytes 1024 | tf_op jit(solution)/shard_map/mlp/pallas_call | solution.py:265
  528.1 23.1 %collective-permute-done.33 = bf16[128,4096]{1,0:T(8,128)(2,1)S(1)} collective-permute-done((bf16[128,4096]{1,0:T(8,128)(2,1)S(1)}, bf16[128,4096]{1,0:T(8,128)(2,1)S(1)}, u32[]{:S(2)}, u32[]{:S(2)}) %collective-permute-start.33) | collective-permute-done | bytes 1048608 | tf_op jit(solution)/shard_map/mlp/ppermute | solution.py:419
  570.7 22.4 %mlp.7 = (bf16[512,2752]{1,0:T(8,128)(2,1)}, bf16[512,2752]{1,0:T(8,128)(2,1)}) custom-call(bf16[512,4096]{1,0:T(8,128)(2,1)} %pad_maximum_fusion.2.rows_ref.refs_1_, bf16[2752,4096]{1,0:T(8,128)(2,1)} %all-gather.14.cloned.1.call-done.down_ref, f32[512,2752]{1,0:T(8,128)} %get-tuple-element.236.gate_ref, f32[512,2752]{1,0:T(8,128)} %get-tuple-element.237.up_ref), custom_call_target="tpu_custom_call" | custom-call | flops 1024 | bytes 1024 | tf_op jit(solution)/shard_map/mlp/pallas_call | solution.py:287
  593.0 33.1 %mlp.8 = bf16[512,4096]{1,0:T(8,128)(2,1)} custom-call(bf16[512,2752]{1,0:T(8,128)(2,1)} %get-tuple-element.250.first_ref.refs_3_, bf16[512,2752]{1,0:T(8,128)(2,1)} %get-tuple-element.249.second_ref.refs_3_, bf16[4096,2752]{1,0:T(8,128)(2,1)} %all-gather.10.cloned.1.call-done.gate_ref.left_ref, bf16[4096,2752]{1,0:T(8,128)(2,1)} %all-gather.12.cloned.1.call-done.up_ref.right_ref), custom_call_target="tpu_custom_call" | custom-call | flops 1024 | bytes 1024 | tf_op jit(solution)/shard_map/mlp/pallas_call | solution.py:312
  633.7 32.4 %mlp.9 = (bf16[512,2752]{1,0:T(8,128)(2,1)}, f32[512,2752]{1,0:T(8,128)}, f32[512,2752]{1,0:T(8,128)}) custom-call(bf16[512,4096]{1,0:T(8,128)(2,1)} %pad_maximum_fusion.1.rows_ref.refs_2_, bf16[4096,2752]{1,0:T(8,128)(2,1)} %all-gather.10.cloned.1.call-done.gate_ref.left_ref, bf16[4096,2752]{1,0:T(8,128)(2,1)} %all-gather.12.cloned.1.call-done.up_ref.right_ref), custom_call_target="tpu_custom_call" | custom-call | flops 1024 | bytes 1024 | tf_op jit(solution)/shard_map/mlp/pallas_call | solution.py:265
  702.6 22.4 %mlp.11 = (bf16[512,2752]{1,0:T(8,128)(2,1)}, bf16[512,2752]{1,0:T(8,128)(2,1)}) custom-call(bf16[512,4096]{1,0:T(8,128)(2,1)} %pad_maximum_fusion.3.refs_2_.rows_ref, bf16[2752,4096]{1,0:T(8,128)(2,1)} %all-gather.14.cloned.1.call-done.down_ref, f32[512,2752]{1,0:T(8,128)} %get-tuple-element.255.gate_ref, f32[512,2752]{1,0:T(8,128)} %get-tuple-element.256.up_ref), custom_call_target="tpu_custom_call" | custom-call | flops 1024 | bytes 1024 | tf_op jit(solution)/shard_map/mlp/pallas_call | solution.py:287
  740.3 33.0 %grads_mlp.6 = bf16[512,4096]{1,0:T(8,128)(2,1)} custom-call(bf16[512,2752]{1,0:T(8,128)(2,1)} %get-tuple-element.271.first_ref.refs_4_, bf16[512,2752]{1,0:T(8,128)(2,1)} %get-tuple-element.268.second_ref.refs_4_, bf16[4096,2752]{1,0:T(8,128)(2,1)} %all-gather.10.cloned.1.call-done.gate_ref.left_ref, ...), custom_call_target="tpu_custom_call" | custom-call | flops 1024 | bytes 1024 | tf_op jit(solution)/shard_map/grads_mlp/pallas_call | solution.py:312
  788.4 19.2 %grads_mlp.7 = bf16[2048,2816]{1,0:T(8,128)(2,1)} custom-call(s32[4]{0:T(128)} %fusion.13.refs_0_, bf16[512,4096]{1,0:T(8,128)(2,1)} %pad_maximum_fusion.2.rows_ref.refs_1_, bf16[512,4096]{1,0:T(8,128)(2,1)} %pad_maximum_fusion.3.refs_2_.rows_ref, bf16[512,2752]{1,0:T(8,128)(2,1)} %get-tuple-element.235.refs_3_, ...), custom_call_target="tpu_custom_call" | custom-call | flops 1024 | bytes 1024 | tf_op jit(solution)/shard_map/grads_mlp/pallas_call | solution.py:178
  889.9 19.3 %grads_mlp.10 = bf16[2048,2816]{1,0:T(8,128)(2,1)} custom-call(s32[4]{0:T(128)} %fusion.13.refs_0_, bf16[512,4096]{1,0:T(8,128)(2,1)} %pad_maximum_fusion.rows_ref.refs_1_, bf16[512,4096]{1,0:T(8,128)(2,1)} %pad_maximum_fusion.1.rows_ref.refs_2_, bf16[512,2752]{1,0:T(8,128)(2,1)} %get-tuple-element.250.first_ref.refs_3_, ...), custom_call_target="tpu_custom_call" | custom-call | flops 1024 | bytes 1024 | tf_op jit(solution)/shard_map/grads_mlp/pallas_call | solution.py:178
  941.4 19.4 %grads_mlp.11 = bf16[2048,2816]{1,0:T(8,128)(2,1)} custom-call(s32[4]{0:T(128)} %fusion.13.refs_0_, bf16[512,4096]{1,0:T(8,128)(2,1)} %pad_maximum_fusion.rows_ref.refs_1_, bf16[512,4096]{1,0:T(8,128)(2,1)} %pad_maximum_fusion.1.rows_ref.refs_2_, bf16[512,2752]{1,0:T(8,128)(2,1)} %get-tuple-element.249.second_ref.refs_3_, ...), custom_call_target="tpu_custom_call" | custom-call | flops 1024 | bytes 1024 | tf_op jit(solution)/shard_map/grads_mlp/pallas_call | solution.py:178
  968.9 29.1 %fusion.35 = f32[1024,4096]{1,0:T(8,128)S(1)} fusion(bf16[1024,2752]{1,0:T(8,128)(2,1)} %slice_dynamic-update-slice_fusion, bf16[2752,4096]{1,0:T(8,128)(2,1)} %all-gather.14.cloned.1.call-done.down_ref), kind=kOutput, calls=%fused_computation.149 | convolution fusion | flops 23085449216 | bytes 44957696 | tf_op jit(solution)/shard_map/grads_mlp/dot_general | solution.py:21
  1045.0 24.4 %d_attn.1.refs_2_ = bf16[1024,3072]{1,0:T(8,128)(2,1)} custom-call(bf16[1024,3072]{1,0:T(8,128)(2,1)} %get-tuple-element.310.kept_ref, bf16[1024,1024]{1,0:T(8,128)(2,1)} %get-tuple-element.198.out_ref, bf16[1024,1024]{1,0:T(8,128)(2,1)} %copy-done.23, f32[1024,128]{1,0:T(8,128)} %get-tuple-element.315.lse_ref, f32[1024,128]{1,0:T(8,128)} %pad_maximum_fusion.8.cos_ref, ...), custom_call_target="tpu_custom_call" | custom-call | flops 1024 | bytes 1024 | tf_op jit(solution)/shard_map/d_attn/pallas_call | solution.py:140
  1069.4 19.4 %grads_attn.8 = bf16[2048,3072]{1,0:T(8,128)(2,1)} custom-call(s32[4]{0:T(128)} %fusion.14.refs_0_, bf16[1024,4096]{1,0:T(8,128)(2,1)} %select_dynamic-update-slice_fusion.refs_1_, bf16[1024,3072]{1,0:T(8,128)(2,1)} %d_attn.1.refs_2_), custom_call_target="tpu_custom_call" | custom-call | flops 1024 | bytes 1024 | tf_op jit(solution)/shard_map/grads_attn/pallas_call | solution.py:178
  1114.1 20.5 %grads_attn.10 = bf16[2048,3072]{1,0:T(8,128)(2,1)} custom-call(s32[4]{0:T(128)} %fusion.13.refs_0_, bf16[1024,4096]{1,0:T(8,128)(2,1)} %select_dynamic-update-slice_fusion.refs_1_, bf16[1024,3072]{1,0:T(8,128)(2,1)} %d_attn.1.refs_2_, bf16[2048,3072]{1,0:T(8,128)(2,1)} %collective-permute-done.67.refs_3_), custom_call_target="tpu_custom_call" | custom-call | flops 1024 | bytes 1024 | tf_op jit(solution)/shard_map/grads_attn/pallas_call | solution.py:178
  1162.2 31.6 %fusion.37 = f32[1024,4096]{1,0:T(8,128)} fusion(bf16[1024,3072]{1,0:T(8,128)(2,1)S(1)} %bitcast.25, bf16[4096,3072]{1,0:T(8,128)(2,1)} %all-gather.6.cloned.1.call-done), kind=kOutput, calls=%fused_computation.151 | convolution fusion | flops 25769803776 | bytes 48234496 | tf_op jit(solution)/shard_map/d_norm_attn/dot_general | solution.py:32
  1232.3 22.2 %collective-permute-done.70 = bf16[256,4096]{1,0:T(8,128)(2,1)} collective-permute-done((bf16[256,4096]{1,0:T(8,128)(2,1)}, bf16[256,4096]{1,0:T(8,128)(2,1)}, u32[]{:S(2)}, u32[]{:S(2)}) %collective-permute-start.70) | collective-permute-done | bytes 2097184 | tf_op jit(solution)/shard_map/d_norm_attn/ppermute | solution.py:442
  1289.9 19.0 %collective-permute-done.72 = bf16[256,4096]{1,0:T(8,128)(2,1)S(1)} collective-permute-done((bf16[256,4096]{1,0:T(8,128)(2,1)}, bf16[256,4096]{1,0:T(8,128)(2,1)S(1)}, u32[]{:S(2)}, u32[]{:S(2)}) %collective-permute-start.72) | collective-permute-done | bytes 2097184 | tf_op jit(solution)/shard_map/grads_attn/ppermute | solution.py:442
  1351.0 26.0 %collective-permute-done.77 = bf16[256,4096]{1,0:T(8,128)(2,1)} collective-permute-done((bf16[256,4096]{1,0:T(8,128)(2,1)}, bf16[256,4096]{1,0:T(8,128)(2,1)}, u32[]{:S(2)}, u32[]{:S(2)}) %collective-permute-start.77) | collective-permute-done | bytes 2097184 | tf_op jit(solution)/shard_map/grads_attn/ppermute | solution.py:442
  (427 shorter events, 727.8 us)
Async XLA Ops:
  7.2 195.7 %all-gather.6.cloned.1.call-start = ((), (), s32[]{:S(2)}) async-start(), calls=%async_computation.5 | async-start | bytes 28311552 | tf_op jit(solution)/shard_map/all_gather | solution.py:534
  13.7 262.1 %all-gather.8.cloned.1.call-start = ((), (), s32[]{:S(2)}) async-start(), calls=%async_computation.6 | async-start | bytes 9437184 | tf_op jit(solution)/shard_map/all_gather | solution.py:535
  14.4 331.2 %all-gather.10.cloned.1.call-start = ((), (), s32[]{:S(2)}) async-start(), calls=%async_computation.7 | async-start | bytes 25952256 | tf_op jit(solution)/shard_map/all_gather | solution.py:536
  18.4 437.5 %all-gather.12.cloned.1.call-start = ((), (), s32[]{:S(2)}) async-start(), calls=%async_computation.8 | async-start | bytes 25952256 | tf_op jit(solution)/shard_map/all_gather | solution.py:537
  23.2 547.5 %all-gather.14.cloned.1.call-start = ((), (), s32[]{:S(2)}) async-start(), calls=%async_computation.9 | async-start | bytes 25362432 | tf_op jit(solution)/shard_map/resid/all_gather | solution.py:589
  32.6 49.9 %collective-permute-start = (bf16[256,4096]{1,0:T(8,128)(2,1)S(1)}, bf16[256,4096]{1,0:T(8,128)(2,1)S(1)}, u32[]{:S(2)}, u32[]{:S(2)}) collective-permute-start(bf16[256,4096]{1,0:T(8,128)(2,1)S(1)} %get-tuple-element.376), channel_id=1, source_target_pairs={{0,1},{1,2},{2,3},{4,5},{5,6},{6,7},{8,9},{9,10},{10,11},{12,13},{... | collective-permute-start | bytes 6291464 | tf_op jit(solution)/shard_map/normed_rows/ppermute | solution.py:419
  37.9 48.9 %collective-permute-start.1 = (bf16[256,4096]{1,0:T(8,128)(2,1)S(1)}, bf16[256,4096]{1,0:T(8,128)(2,1)S(1)}, u32[]{:S(2)}, u32[]{:S(2)}) collective-permute-start(bf16[256,4096]{1,0:T(8,128)(2,1)S(1)} %get-tuple-element.376), channel_id=1, source_target_pairs={{1,0},{2,1},{3,2},{5,4},{6,5},{7,6},{9,8},{10,9},{11,10},{13,12},{... | collective-permute-start | bytes 6291464 | tf_op jit(solution)/shard_map/normed_rows/ppermute | solution.py:419
  88.8 50.6 %collective-permute-start.3 = (bf16[256,4096]{1,0:T(8,128)(2,1)S(1)}, bf16[256,4096]{1,0:T(8,128)(2,1)}, u32[]{:S(2)}, u32[]{:S(2)}) collective-permute-start(bf16[256,4096]{1,0:T(8,128)(2,1)S(1)} %collective-permute-done.1), channel_id=1, source_target_pairs={{1,0},{2,1},{5,4},{6,5},{9,8},{10,9},{13,12},{14,13},{17,16},{18,1... | collective-permute-start | bytes 6291464 | tf_op jit(solution)/shard_map/normed_rows/ppermute | solution.py:419
  141.4 47.6 %collective-permute-start.5 = (bf16[256,4096]{1,0:T(8,128)(2,1)}, bf16[256,4096]{1,0:T(8,128)(2,1)}, u32[]{:S(2)}, u32[]{:S(2)}) collective-permute-start(bf16[256,4096]{1,0:T(8,128)(2,1)} %collective-permute-done.3), channel_id=1, source_target_pairs={{1,0},{5,4},{9,8},{13,12},{17,16},{21,20},{25,24},{29,28}} | collective-permute-start | bytes 6291464 | tf_op jit(solution)/shard_map/normed_rows/ppermute | solution.py:419
  345.6 579.6 %reduce-scatter.6.cloned.1.call-start = ((), (), s32[]{:S(2)}) async-start(), calls=%async_computation.10 | async-start | bytes 14417920 | tf_op jit(solution)/shard_map/grads_mlp/reduce_scatter | solution.py:484
  699.8 88.6 %collective-permute-start.48 = (bf16[2048,2816]{1,0:T(8,128)(2,1)}, bf16[2048,2816]{1,0:T(8,128)(2,1)}, u32[]{:S(2)}, u32[]{:S(2)}) collective-permute-start(bf16[2048,2816]{1,0:T(8,128)(2,1)} %mlp.10), channel_id=1, source_target_pairs={{0,4},{4,0},{8,12},{12,8},{16,20},{20,16},{24,28},{28,24},{1,5},{5... | collective-permute-start | bytes 34603016 | tf_op jit(solution)/shard_map/mlp/ppermute | solution.py:476
  810.9 229.5 %reduce-scatter.8.cloned.1.call-start = ((), (), s32[]{:S(2)}) async-start(), calls=%async_computation.11 | async-start | bytes 14417920 | tf_op jit(solution)/shard_map/grads_mlp/reduce_scatter | solution.py:484
  885.5 55.9 %collective-permute-start.60 = (bf16[2048,2816]{1,0:T(8,128)(2,1)}, bf16[2048,2816]{1,0:T(8,128)(2,1)}, u32[]{:S(2)}, u32[]{:S(2)}) collective-permute-start(bf16[2048,2816]{1,0:T(8,128)(2,1)} %grads_mlp.9), channel_id=1, source_target_pairs={{0,4},{4,0},{8,12},{12,8},{16,20},{20,16},{24,28},{28,24},{1,5},{5... | collective-permute-start | bytes 34603016 | tf_op jit(solution)/shard_map/grads_mlp/ppermute | solution.py:476
  925.2 284.1 %reduce-scatter.10.cloned.1.call-start = ((), (), s32[]{:S(2)}) async-start(), calls=%async_computation.12 | async-start | bytes 14417920 | tf_op jit(solution)/shard_map/d_attn/reduce_scatter | solution.py:484
  965.6 51.8 %collective-permute-start.61 = (bf16[128,4096]{1,0:T(8,128)(2,1)S(1)}, bf16[128,4096]{1,0:T(8,128)(2,1)}, u32[]{:S(2)}, u32[]{:S(2)}) collective-permute-start(bf16[128,4096]{1,0:T(8,128)(2,1)S(1)} %collective-permute-done.58), channel_id=1, source_target_pairs={{2,3},{6,7},{10,11},{14,15},{18,19},{22,23},{26,27},{30,31}} | collective-permute-start | bytes 3145736 | tf_op jit(solution)/shard_map/grads_mlp/ppermute | solution.py:419
  967.2 50.1 %collective-permute-start.62 = (bf16[128,4096]{1,0:T(8,128)(2,1)}, bf16[128,4096]{1,0:T(8,128)(2,1)}, u32[]{:S(2)}, u32[]{:S(2)}) collective-permute-start(bf16[128,4096]{1,0:T(8,128)(2,1)} %collective-permute-done.59), channel_id=1, source_target_pairs={{1,0},{5,4},{9,8},{13,12},{17,16},{21,20},{25,24},{29,28}} | collective-permute-start | bytes 3145736 | tf_op jit(solution)/shard_map/grads_mlp/ppermute | solution.py:419
  1040.5 290.8 %reduce-scatter.12.cloned.1.call-start = ((), (), s32[]{:S(2)}) async-start(), calls=%async_computation.13 | async-start | bytes 15728640 | tf_op jit(solution)/shard_map/grads_attn/reduce_scatter | solution.py:484
  1040.5 48.6 %collective-permute-start.63 = (bf16[256,4096]{1,0:T(8,128)(2,1)}, bf16[256,4096]{1,0:T(8,128)(2,1)S(1)}, u32[]{:S(2)}, u32[]{:S(2)}) collective-permute-start(bf16[256,4096]{1,0:T(8,128)(2,1)} %get-tuple-element.308), channel_id=1, source_target_pairs={{0,1},{4,5},{8,9},{12,13},{16,17},{20,21},{24,25},{28,29}} | collective-permute-start | bytes 6291464 | tf_op jit(solution)/shard_map/grads_mlp/ppermute | solution.py:442
  1094.6 50.1 %collective-permute-start.65 = (bf16[256,4096]{1,0:T(8,128)(2,1)}, bf16[256,4096]{1,0:T(8,128)(2,1)}, u32[]{:S(2)}, u32[]{:S(2)}) collective-permute-start(bf16[256,4096]{1,0:T(8,128)(2,1)} %get-tuple-element.319), channel_id=1, source_target_pairs={{0,1},{1,2},{4,5},{5,6},{8,9},{9,10},{12,13},{13,14},{16,17},{17,1... | collective-permute-start | bytes 6291464 | tf_op jit(solution)/shard_map/grads_attn/ppermute | solution.py:442
  1150.8 53.0 %collective-permute-start.68 = (bf16[256,4096]{1,0:T(8,128)(2,1)S(1)}, bf16[256,4096]{1,0:T(8,128)(2,1)}, u32[]{:S(2)}, u32[]{:S(2)}) collective-permute-start(bf16[256,4096]{1,0:T(8,128)(2,1)S(1)} %get-tuple-element.326), channel_id=1, source_target_pairs={{0,1},{1,2},{2,3},{4,5},{5,6},{6,7},{8,9},{9,10},{10,11},{12,13},{... | collective-permute-start | bytes 6291464 | tf_op jit(solution)/shard_map/grads_attn/ppermute | solution.py:442
  1160.7 48.6 %collective-permute-start.69 = (bf16[256,4096]{1,0:T(8,128)(2,1)S(1)}, bf16[256,4096]{1,0:T(8,128)(2,1)}, u32[]{:S(2)}, u32[]{:S(2)}) collective-permute-start(bf16[256,4096]{1,0:T(8,128)(2,1)S(1)} %get-tuple-element.327), channel_id=1, source_target_pairs={{1,0},{2,1},{3,2},{5,4},{6,5},{7,6},{9,8},{10,9},{11,10},{13,12},{... | collective-permute-start | bytes 6291464 | tf_op jit(solution)/shard_map/grads_attn/ppermute | solution.py:443
  1209.4 184.3 %reduce-scatter.14.cloned.1.call-start = ((), (), s32[]{:S(2)}) async-start(), calls=%async_computation.14 | async-start | bytes 5242880 | tf_op jit(solution)/shard_map/grads_attn/reduce_scatter | solution.py:484
  1334.7 47.7 %collective-permute-start.78 = (bf16[256,4096]{1,0:T(8,128)(2,1)}, bf16[256,4096]{1,0:T(8,128)(2,1)}, u32[]{:S(2)}, u32[]{:S(2)}) collective-permute-start(bf16[256,4096]{1,0:T(8,128)(2,1)} %get-tuple-element.349), channel_id=1, source_target_pairs={{1,0},{2,1},{3,2},{5,4},{6,5},{7,6},{9,8},{10,9},{11,10},{13,12},{... | collective-permute-start | bytes 6291464 | tf_op jit(solution)/shard_map/grads_attn/ppermute | solution.py:443
  1343.5 49.5 %collective-permute-start.81 = (f32[2,4096]{1,0:T(2,128)S(1)}, f32[2,4096]{1,0:T(2,128)S(1)}, u32[]{:S(2)}, u32[]{:S(2)}) collective-permute-start(f32[2,4096]{1,0:T(2,128)S(1)} %add.350), channel_id=1, source_target_pairs={{0,2},{1,3},{2,0},{3,1},{4,6},{5,7},{6,4},{7,5},{8,10},{9,11},{10,... | collective-permute-start | bytes 98312 | tf_op jit(solution)/shard_map/grads_attn/ppermute | solution.py:503
  (128 other events, 3357.0 us)
Sparse Core Ops, SparseCore 0:
  13.8 128.0 all-gather.5
  143.7 55.9 all-gather.7
  202.2 116.4 all-gather.9
  320.4 116.4 all-gather.11
  438.6 118.6 all-gather.13
  811.1 114.0 reduce-scatter.5
  928.3 112.0 reduce-scatter.7
  1043.5 112.0 reduce-scatter.9
  1209.5 118.4 reduce-scatter.11
  1331.4 52.0 reduce-scatter.13

commit v4 on v3

--- a/solution.py
+++ b/solution.py
@@ -544,7 +544,7 @@
         attn_scale = lax.rsqrt(jnp.mean(x_float * x_float, axis=1, keepdims=True) + EPSILON)
         attn_normed = order.mark((x_float * attn_scale * gain_attn).astype(BF16))
         ring = Gather(line, order, attn_normed).step()
-        whole_attn = order.mark(line.in_order(ring.finish()))
+        attn_rows = ring.finish()
     cos, sin = rope_tables(positions)
 
     with jax.named_scope("live_rows"):
@@ -552,6 +552,7 @@
         live = (first_live + jnp.arange(tok_rows) < group_token_counts[0]).astype(BF16)
         live_grad = out_grad * live[:, None]
         live_ring = Gather(line, order, order.after(live_grad)).step()
+        whole_attn = order.mark(line.in_order(attn_rows))
 
     with jax.named_scope("attention"):
         qkv = timed(matmul, whole_attn, qkv_all)

time: 1420 us -> 1410 us (level)
    ppermute x18, waiting for transfers between devices: 215 us -> 201 us  [send(): lax.ppermute(self.high[-1], axis, down)]
  transfers between devices with their start and end apart: 92 -> 92, of which waited for: 40 -> 38; matrix products, arithmetic and copies ran while one was open for 22% -> 22% of each run, Pallas kernels for 26% -> 27%
where the time goes in v4:
time: 1410 us; the launch traced here: 1400 us
  Pallas kernels  438 us (31%)
  waiting for transfers between devices  437 us (31%)
  starting transfers between devices  181 us (13%)
  other arithmetic  141 us (10%)
  matrix products  131 us (9%)
  local copies, waits for them, and re-layouts  52.8 us (4%)
  between operations  16.6 us (1%)
    ppermute x18, waiting for transfers between devices, send(): lax.ppermute(self.high[-1], axis, down)  201 us
    pallas_call x10, Pallas kernels, weight_grad(): pl.pallas_call(lambda *refs: weight_grad_kernel(len(lefts), added is not...  173 us
    ppermute x18, waiting for transfers between devices, send(): low = lax.ppermute(rise, axis, [(k, k + 1) for k in range(step)])  120 us
    ppermute x18, starting transfers between devices, send(): low = lax.ppermute(rise, axis, [(k, k + 1) for k in range(step)])  84 us
    dot_general x4, matrix products, matmul(): return jnp.dot(left, right, preferred_element_type=F32)  77.4 us
    pallas_call x2, Pallas kernels, pair_product(): pl.pallas_call(pair_kernel, grid=(width // TILE,), in_specs=[whole, whole...  66.1 us
    pallas_call x2, Pallas kernels, mlp_forward(): pl.pallas_call(mlp_forward_kernel, grid=(pl.cdiv(width, TILE),), in_specs...  66 us
    ppermute x18, waiting for transfers between devices, send(): lax.ppermute(self.low[-1], axis, up)  63.4 us
  transfers between devices with their start and end apart: 92, of which 38 were waited for; matrix products, arithmetic and copies ran while one was open for 22% of the time, Pallas kernels for 27%

profile of v4, /device:TPU:0, one launch (start us, length us, event | category | flops | bytes accessed | tf_op | source)
XLA Modules:
  0.0 1396.2 jit_solution(4264755427548821881)
XLA Ops:
  39.2 43.3 %collective-permute-done = bf16[256,4096]{1,0:T(8,128)(2,1)S(1)} collective-permute-done((bf16[256,4096]{1,0:T(8,128)(2,1)S(1)}, bf16[256,4096]{1,0:T(8,128)(2,1)S(1)}, u32[]{:S(2)}, u32[]{:S(2)}) %collective-permute-start) | collective-permute-done | bytes 2097184 | tf_op jit(solution)/shard_map/normed_rows/ppermute | solution.py:419
  90.1 49.3 %collective-permute-done.3 = bf16[256,4096]{1,0:T(8,128)(2,1)} collective-permute-done((bf16[256,4096]{1,0:T(8,128)(2,1)S(1)}, bf16[256,4096]{1,0:T(8,128)(2,1)}, u32[]{:S(2)}, u32[]{:S(2)}) %collective-permute-start.3) | collective-permute-done | bytes 2097184 | tf_op jit(solution)/shard_map/normed_rows/ppermute | solution.py:419
  150.2 38.8 %collective-permute-done.5 = bf16[256,4096]{1,0:T(8,128)(2,1)} collective-permute-done((bf16[256,4096]{1,0:T(8,128)(2,1)}, bf16[256,4096]{1,0:T(8,128)(2,1)}, u32[]{:S(2)}, u32[]{:S(2)}) %collective-permute-start.5) | collective-permute-done | bytes 2097184 | tf_op jit(solution)/shard_map/normed_rows/ppermute | solution.py:419
  203.1 33.8 %fusion.32.qkv_ref = f32[1024,3072]{1,0:T(8,128)} fusion(bf16[1024,4096]{1,0:T(8,128)(2,1)} %select_dynamic-update-slice_fusion.refs_1_, bf16[4096,3072]{1,0:T(8,128)(2,1)} %all-gather.6.cloned.1.call-done), kind=kOutput, calls=%fused_computation.146 | convolution fusion | flops 25769803776 | bytes 46137344 | tf_op jit(solution)/shard_map/attention/dot_general | solution.py:21
  241.8 21.7 %attention.1 = (bf16[1024,1024]{1,0:T(8,128)(2,1)}, bf16[1024,3072]{1,0:T(8,128)(2,1)}, f32[1024,128]{1,0:T(8,128)}) custom-call(f32[1024,3072]{1,0:T(8,128)} %fusion.32.qkv_ref, f32[1024,128]{1,0:T(8,128)} %pad_maximum_fusion.8.cos_ref, f32[1024,128]{1,0:T(8,128)} %pad_maximum_fusion.9.sin_ref, s32[1024,1]{1,0:T(8,128)} %copy.27.segr_ref, s32[1,1024]{1,0:T(1,128)} %bitcast.36), custom_call_target="tpu_custom_call" | custom-call | flops 1024 | bytes 1024 | tf_op jit(solution)/shard_map/attention/pallas_call | solution.py:122
  312.7 23.4 %collective-permute-done.15 = bf16[256,4096]{1,0:T(8,128)(2,1)} collective-permute-done((bf16[256,4096]{1,0:T(8,128)(2,1)}, bf16[256,4096]{1,0:T(8,128)(2,1)}, u32[]{:S(2)}, u32[]{:S(2)}) %collective-permute-start.15) | collective-permute-done | bytes 2097184 | tf_op jit(solution)/shard_map/resid/ppermute | solution.py:419
  446.7 33.6 %mlp.6 = (bf16[512,2752]{1,0:T(8,128)(2,1)}, f32[512,2752]{1,0:T(8,128)}, f32[512,2752]{1,0:T(8,128)}) custom-call(bf16[512,4096]{1,0:T(8,128)(2,1)} %pad_maximum_fusion.rows_ref.refs_1_, bf16[4096,2752]{1,0:T(8,128)(2,1)} %all-gather.10.cloned.1.call-done.gate_ref.left_ref, bf16[4096,2752]{1,0:T(8,128)(2,1)} %all-gather.12.cloned.1.call-done.up_ref.right_ref), custom_call_target="tpu_custom_call" | custom-call | flops 1024 | bytes 1024 | tf_op jit(solution)/shard_map/mlp/pallas_call | solution.py:265
  557.3 22.3 %mlp.7 = (bf16[512,2752]{1,0:T(8,128)(2,1)}, bf16[512,2752]{1,0:T(8,128)(2,1)}) custom-call(bf16[512,4096]{1,0:T(8,128)(2,1)} %pad_maximum_fusion.2.rows_ref.refs_1_, bf16[2752,4096]{1,0:T(8,128)(2,1)} %all-gather.14.cloned.1.call-done.down_ref, f32[512,2752]{1,0:T(8,128)} %get-tuple-element.236.gate_ref, f32[512,2752]{1,0:T(8,128)} %get-tuple-element.237.up_ref), custom_call_target="tpu_custom_call" | custom-call | flops 1024 | bytes 1024 | tf_op jit(solution)/shard_map/mlp/pallas_call | solution.py:287
  579.7 33.1 %mlp.8 = bf16[512,4096]{1,0:T(8,128)(2,1)} custom-call(bf16[512,2752]{1,0:T(8,128)(2,1)} %get-tuple-element.250.first_ref.refs_3_, bf16[512,2752]{1,0:T(8,128)(2,1)} %get-tuple-element.249.second_ref.refs_3_, bf16[4096,2752]{1,0:T(8,128)(2,1)} %all-gather.10.cloned.1.call-done.gate_ref.left_ref, bf16[4096,2752]{1,0:T(8,128)(2,1)} %all-gather.12.cloned.1.call-done.up_ref.right_ref), custom_call_target="tpu_custom_call" | custom-call | flops 1024 | bytes 1024 | tf_op jit(solution)/shard_map/mlp/pallas_call | solution.py:312
  622.3 32.4 %mlp.9 = (bf16[512,2752]{1,0:T(8,128)(2,1)}, f32[512,2752]{1,0:T(8,128)}, f32[512,2752]{1,0:T(8,128)}) custom-call(bf16[512,4096]{1,0:T(8,128)(2,1)} %pad_maximum_fusion.1.rows_ref.refs_2_, bf16[4096,2752]{1,0:T(8,128)(2,1)} %all-gather.10.cloned.1.call-done.gate_ref.left_ref, bf16[4096,2752]{1,0:T(8,128)(2,1)} %all-gather.12.cloned.1.call-done.up_ref.right_ref), custom_call_target="tpu_custom_call" | custom-call | flops 1024 | bytes 1024 | tf_op jit(solution)/shard_map/mlp/pallas_call | solution.py:265
  666.3 18.7 %mlp.10 = bf16[2048,2816]{1,0:T(8,128)(2,1)} custom-call(s32[4]{0:T(128)} %fusion.14.refs_0_, bf16[512,4096]{1,0:T(8,128)(2,1)} %pad_maximum_fusion.2.rows_ref.refs_1_, bf16[512,4096]{1,0:T(8,128)(2,1)} %pad_maximum_fusion.3.refs_2_.rows_ref, bf16[512,2752]{1,0:T(8,128)(2,1)} %get-tuple-element.235.refs_3_, bf16[512,2752]{1,0:T(8,128)(2,1)} %get-tuple-element.254.refs_4_), custom_call_target="tpu_custom_call" | custom-call | flops 1024 | bytes 1024 | tf_op jit(solution)/shard_map/mlp/pallas_call | solution.py:178
  694.8 22.4 %mlp.11 = (bf16[512,2752]{1,0:T(8,128)(2,1)}, bf16[512,2752]{1,0:T(8,128)(2,1)}) custom-call(bf16[512,4096]{1,0:T(8,128)(2,1)} %pad_maximum_fusion.3.refs_2_.rows_ref, bf16[2752,4096]{1,0:T(8,128)(2,1)} %all-gather.14.cloned.1.call-done.down_ref, f32[512,2752]{1,0:T(8,128)} %get-tuple-element.255.gate_ref, f32[512,2752]{1,0:T(8,128)} %get-tuple-element.256.up_ref), custom_call_target="tpu_custom_call" | custom-call | flops 1024 | bytes 1024 | tf_op jit(solution)/shard_map/mlp/pallas_call | solution.py:287
  732.0 33.0 %grads_mlp.6 = bf16[512,4096]{1,0:T(8,128)(2,1)} custom-call(bf16[512,2752]{1,0:T(8,128)(2,1)} %get-tuple-element.271.first_ref.refs_4_, bf16[512,2752]{1,0:T(8,128)(2,1)} %get-tuple-element.268.second_ref.refs_4_, bf16[4096,2752]{1,0:T(8,128)(2,1)} %all-gather.10.cloned.1.call-done.gate_ref.left_ref, ...), custom_call_target="tpu_custom_call" | custom-call | flops 1024 | bytes 1024 | tf_op jit(solution)/shard_map/grads_mlp/pallas_call | solution.py:312
  780.3 19.2 %grads_mlp.7 = bf16[2048,2816]{1,0:T(8,128)(2,1)} custom-call(s32[4]{0:T(128)} %fusion.13.refs_0_, bf16[512,4096]{1,0:T(8,128)(2,1)} %pad_maximum_fusion.2.rows_ref.refs_1_, bf16[512,4096]{1,0:T(8,128)(2,1)} %pad_maximum_fusion.3.refs_2_.rows_ref, bf16[512,2752]{1,0:T(8,128)(2,1)} %get-tuple-element.235.refs_3_, ...), custom_call_target="tpu_custom_call" | custom-call | flops 1024 | bytes 1024 | tf_op jit(solution)/shard_map/grads_mlp/pallas_call | solution.py:178
  881.5 19.4 %grads_mlp.10 = bf16[2048,2816]{1,0:T(8,128)(2,1)} custom-call(s32[4]{0:T(128)} %fusion.13.refs_0_, bf16[512,4096]{1,0:T(8,128)(2,1)} %pad_maximum_fusion.rows_ref.refs_1_, bf16[512,4096]{1,0:T(8,128)(2,1)} %pad_maximum_fusion.1.rows_ref.refs_2_, bf16[512,2752]{1,0:T(8,128)(2,1)} %get-tuple-element.250.first_ref.refs_3_, ...), custom_call_target="tpu_custom_call" | custom-call | flops 1024 | bytes 1024 | tf_op jit(solution)/shard_map/grads_mlp/pallas_call | solution.py:178
  933.3 19.4 %grads_mlp.11 = bf16[2048,2816]{1,0:T(8,128)(2,1)} custom-call(s32[4]{0:T(128)} %fusion.13.refs_0_, bf16[512,4096]{1,0:T(8,128)(2,1)} %pad_maximum_fusion.rows_ref.refs_1_, bf16[512,4096]{1,0:T(8,128)(2,1)} %pad_maximum_fusion.1.rows_ref.refs_2_, bf16[512,2752]{1,0:T(8,128)(2,1)} %get-tuple-element.249.second_ref.refs_3_, ...), custom_call_target="tpu_custom_call" | custom-call | flops 1024 | bytes 1024 | tf_op jit(solution)/shard_map/grads_mlp/pallas_call | solution.py:178
  960.2 29.2 %fusion.35 = f32[1024,4096]{1,0:T(8,128)S(1)} fusion(bf16[1024,2752]{1,0:T(8,128)(2,1)} %slice_dynamic-update-slice_fusion, bf16[2752,4096]{1,0:T(8,128)(2,1)} %all-gather.14.cloned.1.call-done.down_ref), kind=kOutput, calls=%fused_computation.149 | convolution fusion | flops 23085449216 | bytes 44957696 | tf_op jit(solution)/shard_map/grads_mlp/dot_general | solution.py:21
  1036.8 24.4 %d_attn.1.refs_2_ = bf16[1024,3072]{1,0:T(8,128)(2,1)} custom-call(bf16[1024,3072]{1,0:T(8,128)(2,1)} %get-tuple-element.310.kept_ref, bf16[1024,1024]{1,0:T(8,128)(2,1)} %get-tuple-element.198.out_ref, bf16[1024,1024]{1,0:T(8,128)(2,1)} %copy-done.23, f32[1024,128]{1,0:T(8,128)} %get-tuple-element.315.lse_ref, f32[1024,128]{1,0:T(8,128)} %pad_maximum_fusion.8.cos_ref, ...), custom_call_target="tpu_custom_call" | custom-call | flops 1024 | bytes 1024 | tf_op jit(solution)/shard_map/d_attn/pallas_call | solution.py:140
  1061.2 19.4 %grads_attn.8 = bf16[2048,3072]{1,0:T(8,128)(2,1)} custom-call(s32[4]{0:T(128)} %fusion.14.refs_0_, bf16[1024,4096]{1,0:T(8,128)(2,1)} %select_dynamic-update-slice_fusion.refs_1_, bf16[1024,3072]{1,0:T(8,128)(2,1)} %d_attn.1.refs_2_), custom_call_target="tpu_custom_call" | custom-call | flops 1024 | bytes 1024 | tf_op jit(solution)/shard_map/grads_attn/pallas_call | solution.py:178
  1105.8 20.5 %grads_attn.10 = bf16[2048,3072]{1,0:T(8,128)(2,1)} custom-call(s32[4]{0:T(128)} %fusion.13.refs_0_, bf16[1024,4096]{1,0:T(8,128)(2,1)} %select_dynamic-update-slice_fusion.refs_1_, bf16[1024,3072]{1,0:T(8,128)(2,1)} %d_attn.1.refs_2_, bf16[2048,3072]{1,0:T(8,128)(2,1)} %collective-permute-done.67.refs_3_), custom_call_target="tpu_custom_call" | custom-call | flops 1024 | bytes 1024 | tf_op jit(solution)/shard_map/grads_attn/pallas_call | solution.py:178
  1154.1 31.6 %fusion.37 = f32[1024,4096]{1,0:T(8,128)} fusion(bf16[1024,3072]{1,0:T(8,128)(2,1)S(1)} %bitcast.25, bf16[4096,3072]{1,0:T(8,128)(2,1)} %all-gather.6.cloned.1.call-done), kind=kOutput, calls=%fused_computation.151 | convolution fusion | flops 25769803776 | bytes 48234496 | tf_op jit(solution)/shard_map/d_norm_attn/dot_general | solution.py:32
  1224.0 22.2 %collective-permute-done.70 = bf16[256,4096]{1,0:T(8,128)(2,1)} collective-permute-done((bf16[256,4096]{1,0:T(8,128)(2,1)}, bf16[256,4096]{1,0:T(8,128)(2,1)}, u32[]{:S(2)}, u32[]{:S(2)}) %collective-permute-start.70) | collective-permute-done | bytes 2097184 | tf_op jit(solution)/shard_map/d_norm_attn/ppermute | solution.py:442
  1281.6 19.0 %collective-permute-done.72 = bf16[256,4096]{1,0:T(8,128)(2,1)S(1)} collective-permute-done((bf16[256,4096]{1,0:T(8,128)(2,1)}, bf16[256,4096]{1,0:T(8,128)(2,1)S(1)}, u32[]{:S(2)}, u32[]{:S(2)}) %collective-permute-start.72) | collective-permute-done | bytes 2097184 | tf_op jit(solution)/shard_map/grads_attn/ppermute | solution.py:442
  1342.6 26.1 %collective-permute-done.77 = bf16[256,4096]{1,0:T(8,128)(2,1)} collective-permute-done((bf16[256,4096]{1,0:T(8,128)(2,1)}, bf16[256,4096]{1,0:T(8,128)(2,1)}, u32[]{:S(2)}, u32[]{:S(2)}) %collective-permute-start.77) | collective-permute-done | bytes 2097184 | tf_op jit(solution)/shard_map/grads_attn/ppermute | solution.py:442
  (427 shorter events, 723.5 us)
Async XLA Ops:
  7.2 195.9 %all-gather.6.cloned.1.call-start = ((), (), s32[]{:S(2)}) async-start(), calls=%async_computation.5 | async-start | bytes 28311552 | tf_op jit(solution)/shard_map/all_gather | solution.py:534
  13.7 251.8 %all-gather.8.cloned.1.call-start = ((), (), s32[]{:S(2)}) async-start(), calls=%async_computation.6 | async-start | bytes 9437184 | tf_op jit(solution)/shard_map/all_gather | solution.py:535
  14.4 322.4 %all-gather.10.cloned.1.call-start = ((), (), s32[]{:S(2)}) async-start(), calls=%async_computation.7 | async-start | bytes 25952256 | tf_op jit(solution)/shard_map/all_gather | solution.py:536
  18.4 428.3 %all-gather.12.cloned.1.call-start = ((), (), s32[]{:S(2)}) async-start(), calls=%async_computation.8 | async-start | bytes 25952256 | tf_op jit(solution)/shard_map/all_gather | solution.py:537
  23.2 534.2 %all-gather.14.cloned.1.call-start = ((), (), s32[]{:S(2)}) async-start(), calls=%async_computation.9 | async-start | bytes 25362432 | tf_op jit(solution)/shard_map/resid/all_gather | solution.py:590
  32.6 49.9 %collective-permute-start = (bf16[256,4096]{1,0:T(8,128)(2,1)S(1)}, bf16[256,4096]{1,0:T(8,128)(2,1)S(1)}, u32[]{:S(2)}, u32[]{:S(2)}) collective-permute-start(bf16[256,4096]{1,0:T(8,128)(2,1)S(1)} %get-tuple-element.376), channel_id=1, source_target_pairs={{0,1},{1,2},{2,3},{4,5},{5,6},{6,7},{8,9},{9,10},{10,11},{12,13},{... | collective-permute-start | bytes 6291464 | tf_op jit(solution)/shard_map/normed_rows/ppermute | solution.py:419
  37.9 48.9 %collective-permute-start.1 = (bf16[256,4096]{1,0:T(8,128)(2,1)S(1)}, bf16[256,4096]{1,0:T(8,128)(2,1)S(1)}, u32[]{:S(2)}, u32[]{:S(2)}) collective-permute-start(bf16[256,4096]{1,0:T(8,128)(2,1)S(1)} %get-tuple-element.376), channel_id=1, source_target_pairs={{1,0},{2,1},{3,2},{5,4},{6,5},{7,6},{9,8},{10,9},{11,10},{13,12},{... | collective-permute-start | bytes 6291464 | tf_op jit(solution)/shard_map/normed_rows/ppermute | solution.py:419
  88.8 50.6 %collective-permute-start.3 = (bf16[256,4096]{1,0:T(8,128)(2,1)S(1)}, bf16[256,4096]{1,0:T(8,128)(2,1)}, u32[]{:S(2)}, u32[]{:S(2)}) collective-permute-start(bf16[256,4096]{1,0:T(8,128)(2,1)S(1)} %collective-permute-done.1), channel_id=1, source_target_pairs={{1,0},{2,1},{5,4},{6,5},{9,8},{10,9},{13,12},{14,13},{17,16},{18,1... | collective-permute-start | bytes 6291464 | tf_op jit(solution)/shard_map/normed_rows/ppermute | solution.py:419
  188.9 47.9 %collective-permute-start.6 = (bf16[256,4096]{1,0:T(8,128)(2,1)S(1)}, bf16[256,4096]{1,0:T(8,128)(2,1)}, u32[]{:S(2)}, u32[]{:S(2)}) collective-permute-start(bf16[256,4096]{1,0:T(8,128)(2,1)S(1)} %broadcast_multiply_fusion), channel_id=1, source_target_pairs={{0,1},{1,2},{2,3},{4,5},{5,6},{6,7},{8,9},{9,10},{10,11},{12,13},{... | collective-permute-start | bytes 6291464 | tf_op jit(solution)/shard_map/live_rows/ppermute | solution.py:419
  336.8 580.1 %reduce-scatter.6.cloned.1.call-start = ((), (), s32[]{:S(2)}) async-start(), calls=%async_computation.10 | async-start | bytes 14417920 | tf_op jit(solution)/shard_map/grads_mlp/reduce_scatter | solution.py:484
  688.6 91.7 %collective-permute-start.48 = (bf16[2048,2816]{1,0:T(8,128)(2,1)}, bf16[2048,2816]{1,0:T(8,128)(2,1)}, u32[]{:S(2)}, u32[]{:S(2)}) collective-permute-start(bf16[2048,2816]{1,0:T(8,128)(2,1)} %mlp.10), channel_id=1, source_target_pairs={{0,4},{4,0},{8,12},{12,8},{16,20},{20,16},{24,28},{28,24},{1,5},{5... | collective-permute-start | bytes 34603016 | tf_op jit(solution)/shard_map/mlp/ppermute | solution.py:476
  802.7 229.5 %reduce-scatter.8.cloned.1.call-start = ((), (), s32[]{:S(2)}) async-start(), calls=%async_computation.11 | async-start | bytes 14417920 | tf_op jit(solution)/shard_map/grads_mlp/reduce_scatter | solution.py:484
  877.1 56.2 %collective-permute-start.60 = (bf16[2048,2816]{1,0:T(8,128)(2,1)}, bf16[2048,2816]{1,0:T(8,128)(2,1)}, u32[]{:S(2)}, u32[]{:S(2)}) collective-permute-start(bf16[2048,2816]{1,0:T(8,128)(2,1)} %grads_mlp.9), channel_id=1, source_target_pairs={{0,4},{4,0},{8,12},{12,8},{16,20},{20,16},{24,28},{28,24},{1,5},{5... | collective-permute-start | bytes 34603016 | tf_op jit(solution)/shard_map/grads_mlp/ppermute | solution.py:476
  916.9 284.1 %reduce-scatter.10.cloned.1.call-start = ((), (), s32[]{:S(2)}) async-start(), calls=%async_computation.12 | async-start | bytes 14417920 | tf_op jit(solution)/shard_map/d_attn/reduce_scatter | solution.py:484
  957.3 51.5 %collective-permute-start.61 = (bf16[128,4096]{1,0:T(8,128)(2,1)S(1)}, bf16[128,4096]{1,0:T(8,128)(2,1)}, u32[]{:S(2)}, u32[]{:S(2)}) collective-permute-start(bf16[128,4096]{1,0:T(8,128)(2,1)S(1)} %collective-permute-done.58), channel_id=1, source_target_pairs={{2,3},{6,7},{10,11},{14,15},{18,19},{22,23},{26,27},{30,31}} | collective-permute-start | bytes 3145736 | tf_op jit(solution)/shard_map/grads_mlp/ppermute | solution.py:419
  958.9 49.9 %collective-permute-start.62 = (bf16[128,4096]{1,0:T(8,128)(2,1)}, bf16[128,4096]{1,0:T(8,128)(2,1)}, u32[]{:S(2)}, u32[]{:S(2)}) collective-permute-start(bf16[128,4096]{1,0:T(8,128)(2,1)} %collective-permute-done.59), channel_id=1, source_target_pairs={{1,0},{5,4},{9,8},{13,12},{17,16},{21,20},{25,24},{29,28}} | collective-permute-start | bytes 3145736 | tf_op jit(solution)/shard_map/grads_mlp/ppermute | solution.py:419
  1032.2 290.7 %reduce-scatter.12.cloned.1.call-start = ((), (), s32[]{:S(2)}) async-start(), calls=%async_computation.13 | async-start | bytes 15728640 | tf_op jit(solution)/shard_map/grads_attn/reduce_scatter | solution.py:484
  1032.2 48.6 %collective-permute-start.63 = (bf16[256,4096]{1,0:T(8,128)(2,1)}, bf16[256,4096]{1,0:T(8,128)(2,1)S(1)}, u32[]{:S(2)}, u32[]{:S(2)}) collective-permute-start(bf16[256,4096]{1,0:T(8,128)(2,1)} %get-tuple-element.308), channel_id=1, source_target_pairs={{0,1},{4,5},{8,9},{12,13},{16,17},{20,21},{24,25},{28,29}} | collective-permute-start | bytes 6291464 | tf_op jit(solution)/shard_map/grads_mlp/ppermute | solution.py:442
  1086.3 50.1 %collective-permute-start.65 = (bf16[256,4096]{1,0:T(8,128)(2,1)}, bf16[256,4096]{1,0:T(8,128)(2,1)}, u32[]{:S(2)}, u32[]{:S(2)}) collective-permute-start(bf16[256,4096]{1,0:T(8,128)(2,1)} %get-tuple-element.319), channel_id=1, source_target_pairs={{0,1},{1,2},{4,5},{5,6},{8,9},{9,10},{12,13},{13,14},{16,17},{17,1... | collective-permute-start | bytes 6291464 | tf_op jit(solution)/shard_map/grads_attn/ppermute | solution.py:442
  1142.5 52.9 %collective-permute-start.68 = (bf16[256,4096]{1,0:T(8,128)(2,1)S(1)}, bf16[256,4096]{1,0:T(8,128)(2,1)}, u32[]{:S(2)}, u32[]{:S(2)}) collective-permute-start(bf16[256,4096]{1,0:T(8,128)(2,1)S(1)} %get-tuple-element.326), channel_id=1, source_target_pairs={{0,1},{1,2},{2,3},{4,5},{5,6},{6,7},{8,9},{9,10},{10,11},{12,13},{... | collective-permute-start | bytes 6291464 | tf_op jit(solution)/shard_map/grads_attn/ppermute | solution.py:442
  1152.3 48.7 %collective-permute-start.69 = (bf16[256,4096]{1,0:T(8,128)(2,1)S(1)}, bf16[256,4096]{1,0:T(8,128)(2,1)}, u32[]{:S(2)}, u32[]{:S(2)}) collective-permute-start(bf16[256,4096]{1,0:T(8,128)(2,1)S(1)} %get-tuple-element.327), channel_id=1, source_target_pairs={{1,0},{2,1},{3,2},{5,4},{6,5},{7,6},{9,8},{10,9},{11,10},{13,12},{... | collective-permute-start | bytes 6291464 | tf_op jit(solution)/shard_map/grads_attn/ppermute | solution.py:443
  1201.1 184.3 %reduce-scatter.14.cloned.1.call-start = ((), (), s32[]{:S(2)}) async-start(), calls=%async_computation.14 | async-start | bytes 5242880 | tf_op jit(solution)/shard_map/grads_attn/reduce_scatter | solution.py:484
  1326.4 47.7 %collective-permute-start.78 = (bf16[256,4096]{1,0:T(8,128)(2,1)}, bf16[256,4096]{1,0:T(8,128)(2,1)}, u32[]{:S(2)}, u32[]{:S(2)}) collective-permute-start(bf16[256,4096]{1,0:T(8,128)(2,1)} %get-tuple-element.349), channel_id=1, source_target_pairs={{1,0},{2,1},{3,2},{5,4},{6,5},{7,6},{9,8},{10,9},{11,10},{13,12},{... | collective-permute-start | bytes 6291464 | tf_op jit(solution)/shard_map/grads_attn/ppermute | solution.py:443
  1335.1 49.6 %collective-permute-start.81 = (f32[2,4096]{1,0:T(2,128)S(1)}, f32[2,4096]{1,0:T(2,128)S(1)}, u32[]{:S(2)}, u32[]{:S(2)}) collective-permute-start(f32[2,4096]{1,0:T(2,128)S(1)} %add.350), channel_id=1, source_target_pairs={{0,2},{1,3},{2,0},{3,1},{4,6},{5,7},{6,4},{7,5},{8,10},{9,11},{10,... | collective-permute-start | bytes 98312 | tf_op jit(solution)/shard_map/grads_attn/ppermute | solution.py:503
  (128 other events, 3355.6 us)
Sparse Core Ops, SparseCore 0:
  13.8 128.0 all-gather.5
  143.7 55.9 all-gather.7
  202.2 116.4 all-gather.9
  320.4 116.4 all-gather.11
  438.6 118.6 all-gather.13
  802.8 114.0 reduce-scatter.5
  920.0 112.0 reduce-scatter.7
  1035.3 112.0 reduce-scatter.9
  1201.1 118.4 reduce-scatter.11
  1323.1 52.0 reduce-scatter.13
